TPU v7x, 32 devices: a whole 2x2x4 slice. The times are simulated.
32 devices in a mesh: member: 1, lat: 4 (over z), lev: 4 (over y, x), fld: 2 (over core).
Axes of the slice: x: 2, y: 2, z: 4, core: 2. Of those that a mesh axis runs over, the one named last changes fastest.
Arguments:
- grid_state: bfloat16 [2, 16, 2, 512, 2048], P('member', 'lev', 'fld', 'lat'), may hold values from -6 to 6
- legendre: bfloat16 [512, 2, 512, 640], P(('lat', 'lev'), 'fld'), may hold values from -0.25 to 0.25
- pair_order: int32 [512], replicated, may hold values from 0 to 511, each once
- band_start: int32 [1024], replicated, may hold values from 0 to 286
- mode_analysis: float32 [32, 32], replicated, may hold values from -1 to 1
- mode_synthesis: float32 [32, 32], replicated, may hold values from -1 to 1
- mode_rate: float32 [32], replicated, may hold values from 0.05 to 50
Outputs:
- grid_out: bfloat16 [2, 16, 2, 512, 2048], P('member', 'lev', 'fld', 'lat')
Inputs may be any that keep to these rules, and one draw needn't show every extreme that they name: `pair_order`: every value appears once.
All inputs are finite; a program needn't handle non-finite values.
Results may differ from a plain program's by a relative error of at most 0.009.
Values may be sent and summed in bfloat16 or wider, within the bound.
No kernel may reach another device: no remote copies, remote signals or barrier semaphores. Data moves between devices by JAX's collectives and lax.ppermute only.
A program may use at most 128 MiB of HBM per device.

v0:
```python
import functools
import math

import jax
import jax.numpy as jnp
from jax import lax
from jax.experimental import pallas as pl
from jax.experimental.pallas import tpu as pltpu
from jax.sharding import PartitionSpec as P


LANES = 128


def swap_with(value, axis, mask):
    if mask == 0:
        return value
    pairs = [(source, source ^ mask) for source in range(lax.axis_size(axis))]
    return lax.ppermute(value, axis, pairs)


def pick(table, index):
    places = jnp.arange(table.shape[0], dtype=jnp.int32)
    return jnp.sum(jnp.where(index[:, None] == places[None, :], table[None, :], 0), axis=1)


def fold_kernel(state, even, odd):
    half = even.shape[2]
    lats = even.shape[1]
    step = 16 if lats % 16 == 0 else lats

    def products(rows, columns):
        wind_part, heat_part = state[0, 0, 0, rows, columns], state[1, 0, 0, rows, columns]
        wind, heat = wind_part.astype(jnp.float32), heat_part.astype(jnp.float32)
        return wind_part * heat_part, (wind * wind - heat * heat).astype(jnp.bfloat16)

    for top in range(0, lats, step):
        rows = slice(top, top + step)
        for left in range(0, half, LANES):
            columns = slice(left, left + LANES)
            lows = products(rows, columns)
            highs = products(rows, slice(half + left, half + left + LANES))
            for field, (low, high) in enumerate(zip(lows, highs)):
                even[field, rows, columns] = low + high
                odd[field, rows, columns] = low - high


def folded_products(grid_state):
    fields, levels, _, lats, lon_count = grid_state.shape
    half = lon_count // 2
    out = jax.ShapeDtypeStruct((fields, levels * lats, half), jnp.bfloat16)
    even, odd = pl.pallas_call(
        fold_kernel,
        grid=(levels,),
        in_specs=[pl.BlockSpec((fields, 1, 1, lats, lon_count), lambda i: (0, i, 0, 0, 0))],
        out_specs=[pl.BlockSpec((fields, lats, half), lambda i: (0, i, 0))] * 2,
        out_shape=[out, out],
        cost_estimate=pl.CostEstimate(
            flops=grid_state.size * 4, bytes_accessed=grid_state.size * 4, transcendentals=0
        ),
    )(grid_state)
    return even.reshape(-1, half), odd.reshape(-1, half)


def cos_sin(phase, quarter):
    shift = quarter.bit_length() - 1
    quadrant = (phase + quarter // 2) >> shift
    theta = (phase - (quadrant << shift)).astype(jnp.float32) * (0.5 * math.pi / quarter)
    square = theta * theta
    sine = theta * (
        1.0
        + square
        * (-1.0 / 6 + square * (1.0 / 120 + square * (-1.0 / 5040 + square * (1.0 / 362880))))
    )
    cosine = 1.0 + square * (
        -0.5
        + square
        * (1.0 / 24 + square * (-1.0 / 720 + square * (1.0 / 40320 - square * (1.0 / 3628800))))
    )
    swap = (quadrant & 1) == 1
    real = jnp.where(swap, sine, cosine)
    imaginary = jnp.where(swap, cosine, sine)
    real = jnp.where(((quadrant + 1) & 2) == 2, -real, real)
    imaginary = jnp.where((quadrant & 2) == 2, -imaginary, imaginary)
    return real, imaginary


def forward_kernel(waves, even, odd, fourier, table, *, slots, lon_count):
    dists, levs, parities, tall, _ = fourier.shape
    half = even.shape[1]
    scaling = 1.0 / math.sqrt(lon_count)

    @pl.when(pl.program_id(0) == 0)
    def _():
        fine = lax.broadcasted_iota(jnp.int32, (1, LANES), 1)
        for parity in range(parities):
            for dist in range(dists):
                wave = waves[dist, parity]
                c_step, s_step = cos_sin((wave * LANES) & (lon_count - 1), lon_count // 4)
                c_here, s_here = cos_sin((wave * fine) & (lon_count - 1), lon_count // 4)
                c_here, s_here = c_here * scaling, s_here * scaling
                for block in range(half // LANES):
                    there = slice(block * LANES, (block + 1) * LANES)
                    for part, value in enumerate((c_here, -s_here)):
                        value = value.astype(table.dtype)
                        for lev in range(levs):
                            top = (dist * levs + lev) * tall + part * slots
                            table[parity, top : top + slots, there] = value[
                                lev * slots : (lev + 1) * slots
                            ]
                    c_here, s_here = (
                        c_here * c_step - s_here * s_step,
                        s_here * c_step + c_here * s_step,
                    )

    for parity, grid_rows in enumerate((even, odd)):
        sums = lax.dot_general(
            table[parity],
            grid_rows[...],
            (((1,), (1,)), ((), ())),
            preferred_element_type=jnp.float32,
        ).astype(fourier.dtype)
        for dist in range(dists):
            for lev in range(levs):
                top = (dist * levs + lev) * tall
                fourier[dist, lev, parity] = sums[top : top + tall]


def forward_stage(waves, even, odd, slots, lon_count):
    dists, parities, lines, _ = waves.shape
    levs = lines // slots
    rows, half = even.shape
    block = min(rows, 512)
    whole = lambda shape: pl.BlockSpec(shape, lambda i: (0,) * len(shape))
    shape = (dists, levs, parities, 2 * slots, rows)
    table_shape = (parities, dists * levs * 2 * slots, half)
    return pl.pallas_call(
        functools.partial(forward_kernel, slots=slots, lon_count=lon_count),
        grid=(rows // block,),
        in_specs=[whole(waves.shape)] + [pl.BlockSpec((block, half), lambda i: (i, 0))] * 2,
        out_specs=[
            pl.BlockSpec(shape[:-1] + (block,), lambda i: (0, 0, 0, 0, i)),
            whole(table_shape),
        ],
        out_shape=[
            jax.ShapeDtypeStruct(shape, jnp.bfloat16),
            jax.ShapeDtypeStruct(table_shape, jnp.bfloat16),
        ],
        cost_estimate=pl.CostEstimate(
            flops=2 * math.prod(shape) * half,
            bytes_accessed=4 * rows * half + 2 * math.prod(shape) + 2 * math.prod(table_shape),
            transcendentals=0,
        ),
    )(waves, even, odd)


def inverse_kernel(*refs, dists, chunks):
    hemis, tables, out = refs[: dists * chunks], refs[dists * chunks : -1], refs[-1]
    half = tables[0].shape[2]
    sums = []
    for parity in range(2):
        total = None
        for chunk in range(chunks):
            hemi = jnp.concatenate(
                [
                    hemis[chunk * dists + dist][lev, parity]
                    for dist in range(dists)
                    for lev in range(hemis[0].shape[0])
                ],
                axis=0,
            )
            table = tables[chunk][parity]
            part = lax.dot_general(
                hemi, table, (((0,), (0,)), ((), ())), preferred_element_type=jnp.float32
            )
            total = part if total is None else total + part
        sums.append(total)
    out[:, :half] = (sums[0] + sums[1]).astype(out.dtype)
    out[:, half:] = (sums[0] - sums[1]).astype(out.dtype)


def inverse_stage(hemis, tables):
    rows = hemis[0][0].shape[-1]
    half = tables[0].shape[-1]
    dists = len(hemis[0])
    block = min(rows, 256)
    flat = [piece for pieces in hemis for piece in pieces]
    whole = lambda shape: pl.BlockSpec(shape, lambda i: (0,) * len(shape))
    total = sum(piece.size for piece in flat)
    return pl.pallas_call(
        functools.partial(inverse_kernel, dists=dists, chunks=len(hemis)),
        grid=(rows // block,),
        in_specs=[pl.BlockSpec(piece.shape[:3] + (block,), lambda i: (0, 0, 0, i)) for piece in flat]
        + [whole(table.shape) for table in tables],
        out_specs=pl.BlockSpec((block, 2 * half), lambda i: (i, 0)),
        out_shape=jax.ShapeDtypeStruct((rows, 2 * half), jnp.bfloat16),
        cost_estimate=pl.CostEstimate(
            flops=2 * total * half,
            bytes_accessed=2 * total + 2 * sum(t.size for t in tables) + 4 * rows * half,
            transcendentals=0,
        ),
    )(*flat, *tables)


def in_three(matrix):
    high = matrix.astype(jnp.bfloat16)
    low = (matrix - high.astype(jnp.float32)).astype(jnp.bfloat16)
    return jnp.concatenate([high, high, low], axis=1)


def legendre_kernel(
    numbers, *refs, lats, dists, lev_count, wave_count, slots, first_slot, lat_at, together
):
    near, far = refs[:dists], refs[dists : dists + lev_count - 1]
    table, analysis, synthesis, rate, out, work, lines_in = refs[dists + lev_count - 1 :]
    slots_all = lat_at
    slot = pl.program_id(0)
    tall = 2 * slots
    lines = out.shape[4] // lats
    group = lev_count * lines
    rows = 2 * group

    def piece(dist, parity, lev, line):
        there = slice(line * lats, (line + 1) * lats)
        if lev == 0:
            return near[dist][0, parity, :, there]
        return far[lev - 1][dist, parity, :, there]

    def place(dist, parity, lev, line):
        at = (((dist * 2 + parity) * lev_count + lev) * lines + line) * tall
        return slice(at, at + tall)

    every = [
        (dist, parity, lev, line)
        for dist in range(dists)
        for parity in range(2)
        for lev in range(lev_count)
        for line in range(lines)
    ]

    @pl.when(slot == 0)
    def _():
        for at in every:
            work[place(*at), :] = piece(*at).astype(jnp.float32)

    parity_here = numbers[3 * slots_all]
    lat_here = numbers[3 * slots_all + 1]
    cols = table.shape[3]
    column = lax.broadcasted_iota(jnp.int32, (1, cols), 1)
    lane = lax.broadcasted_iota(jnp.int32, (1, lats), 1)

    def rows_at(slot, block, parity, part):
        dist = block ^ lat_here
        at = (dist * 2 + parity) * (group * tall) + part * slots + slot
        return pl.ds(at, group, stride=tall)

    def starts_of(slot):
        at = first_slot + slot
        return [numbers[slots_all + at], numbers[2 * slots_all + at]]

    def gather(slot, lines_in):
        starts = starts_of(slot)
        for block in range(dists):
            for parity in range(2):
                keep = lane + block * lats >= starts[parity]
                for part in range(2):
                    value = work[rows_at(slot, block, parity, part), :]
                    top = parity * rows + part * group
                    lines_in[top : top + group, block * lats : (block + 1) * lats] = jnp.where(
                        keep, value, 0.0
                    ).astype(lines_in.dtype)

    def mix(matrix, value):
        high = value.astype(jnp.bfloat16)
        low = (value - high.astype(jnp.float32)).astype(jnp.bfloat16)
        return jnp.dot(
            matrix[...],
            jnp.concatenate([high, low, high], axis=0),
            preferred_element_type=jnp.float32,
        )

    def transform(slot, lines_in, legendre):
        first = numbers[first_slot + slot]
        second = wave_count - 1 - first
        first_odd = (first & 1) == 1
        count_one = ((wave_count - 1 - first - parity_here) >> 1) + 1
        count_two = jnp.maximum(((first - parity_here) >> 1) + 1, 0)
        degree = jnp.where(
            column < count_one,
            first + parity_here + 2 * column,
            second + parity_here + 2 * (column - count_one),
        )
        even_from = jnp.where(first_odd, count_one, 0)
        even_to = jnp.where(first_odd, count_one + count_two, count_one)
        odd_from = jnp.where(first_odd, 0, count_one)
        odd_to = jnp.where(first_odd, count_one, count_one + count_two)
        in_even = (column >= even_from) & (column < even_to)
        in_odd = (column >= odd_from) & (column < odd_to)
        both = jnp.dot(lines_in[...], legendre[...], preferred_element_type=jnp.float32)
        spectral = jnp.where(in_even, both[:rows], both[rows:])
        level_deg = degree.astype(jnp.float32)
        growth = level_deg * (level_deg + 1.0) / float(wave_count * wave_count)
        factor = 1.0 / (1.0 + growth * rate[...])
        mixed = mix(analysis, spectral).reshape(2, rows // 2, cols)
        coupled = mix(synthesis, (mixed * factor[None]).reshape(rows, cols))
        split = jnp.concatenate(
            [jnp.where(in_even, coupled, 0.0), jnp.where(in_odd, coupled, 0.0)], axis=0
        ).astype(jnp.bfloat16)
        return lax.dot_general(
            split, legendre[...], (((1,), (1,)), ((), ())), preferred_element_type=jnp.float32
        )

    def scatter(slot, back):
        starts = starts_of(slot)
        first = numbers[first_slot + slot]
        even_wave = jnp.where((first & 1) == 1, wave_count - 1 - first, first)
        weights = [jnp.where(even_wave == 0, 1.0, 2.0), 2.0]
        for block in range(dists):
            for parity in range(2):
                keep = lane + block * lats >= starts[parity]
                for part in range(2):
                    top = parity * rows + part * group
                    value = back[top : top + group, block * lats : (block + 1) * lats]
                    work[rows_at(slot, block, parity, part), :] = jnp.where(
                        keep, value * weights[parity], 0.0
                    )

    here = [slot * together + sub for sub in range(together)]
    for sub in range(together):
        gather(here[sub], lines_in.at[sub])
    backs = [transform(here[sub], lines_in.at[sub], table.at[sub, 0]) for sub in range(together)]
    for sub in range(together):
        scatter(here[sub], backs[sub])

    @pl.when(slot == slots // together - 1)
    def _():
        for at in every:
            dist, parity, lev, line = at
            out[lev, dist, parity, :, line * lats : (line + 1) * lats] = work[
                place(*at), :
            ].astype(out.dtype)


def legendre_stage(
    near, far, legendre, numbers, analysis, synthesis, rate, wave_count, lats, slots, first_slot
):
    dists, lev_count = len(near), len(far) + 1
    _, parities, tall, width = near[0].shape
    slots_all, _, lat_total, cols = legendre.shape
    rows = 2 * lev_count * (width // lats)
    together = 2 if slots % 2 == 0 and first_slot % 2 == 0 else 1
    whole = lambda shape: pl.BlockSpec(shape, lambda i, n: (0,) * len(shape))
    shape = (lev_count, dists, parities, tall, width)
    return pl.pallas_call(
        functools.partial(
            legendre_kernel,
            lats=lats,
            dists=dists,
            lev_count=lev_count,
            wave_count=wave_count,
            slots=slots,
            first_slot=first_slot,
            lat_at=slots_all,
            together=together,
        ),
        grid_spec=pltpu.PrefetchScalarGridSpec(
            num_scalar_prefetch=1,
            grid=(slots // together,),
            in_specs=[
                pl.BlockSpec((1, parities, tall, width), lambda i, n: (0, 0, 0, 0)) for _ in near
            ]
            + [whole(piece.shape) for piece in far]
            + [
                pl.BlockSpec(
                    (together, 1, lat_total, cols),
                    lambda i, n: (first_slot // together + i, 0, 0, 0),
                ),
                whole(analysis.shape),
                whole(synthesis.shape),
                whole(rate.shape),
            ],
            out_specs=whole(shape),
            scratch_shapes=[
                pltpu.VMEM((dists * rows * tall, lats), jnp.float32),
                pltpu.VMEM((together, 2 * rows, lat_total), jnp.bfloat16),
            ],
        ),
        out_shape=jax.ShapeDtypeStruct(shape, jnp.bfloat16),
        cost_estimate=pl.CostEstimate(
            flops=slots * (2 * 2 * 2 * rows * lat_total * cols + 2 * 2 * 3 * rows * rows * cols),
            bytes_accessed=slots * lat_total * cols * 2 + 4 * math.prod(shape),
            transcendentals=0,
        ),
    )(numbers, *near, *far, legendre, analysis, synthesis, rate)


def chunk_sizes(slots):
    return [slots // 4] * 4 if slots % 4 == 0 else [slots]


def local(grid_state, legendre, pair_order, band_start, mode_analysis, mode_synthesis, mode_rate):
    lat_count = lax.axis_size("lat")
    lev_count = lax.axis_size("lev")
    lat_here = lax.axis_index("lat")
    lev_here = lax.axis_index("lev")
    parity = lax.axis_index("fld")
    wave_count = band_start.shape[0]
    lon_count = grid_state.shape[-1]
    field_count, levels_here, _, lats_here, _ = grid_state.shape
    slots_here = legendre.shape[0]
    modes_count = mode_rate.shape[0]
    sizes = chunk_sizes(slots_here)
    firsts = [sum(sizes[:chunk]) for chunk in range(len(sizes))]

    indices, odds = [], []
    for first, slots in zip(firsts, sizes):
        shape = (lat_count, 2, lev_count, slots)
        axis = lambda k: lax.broadcasted_iota(jnp.int32, shape, k)
        owner = (axis(0) ^ lat_here) * lev_count + (axis(2) ^ lev_here)
        indices.append((owner * slots_here + first + axis(3)).reshape(-1))
        odds.append(axis(1).reshape(-1))
    pair_at = pick(pair_order, jnp.concatenate(indices))
    odd_at = jnp.concatenate(odds)
    all_waves = jnp.where((pair_at & 1) == odd_at, pair_at, wave_count - 1 - pair_at)
    all_waves = jnp.broadcast_to(all_waves[:, None], (all_waves.shape[0], LANES))

    own_first = lax.dynamic_slice_in_dim(
        pair_order, (lat_here * lev_count + lev_here) * slots_here, slots_here
    )
    first_is_odd = (own_first & 1) == 1
    even_wave = jnp.where(first_is_odd, wave_count - 1 - own_first, own_first)
    own_starts = pick(
        band_start, jnp.concatenate([even_wave, wave_count - 1 - even_wave])
    )
    numbers = jnp.concatenate(
        [own_first, own_starts, jnp.stack([parity, lat_here]).astype(jnp.int32)]
    )

    mode_at = (
        jnp.arange(field_count, dtype=jnp.int32)[None, :, None] * (lev_count * levels_here)
        + (jnp.arange(lev_count, dtype=jnp.int32) ^ lev_here)[:, None, None] * levels_here
        + jnp.arange(levels_here, dtype=jnp.int32)[None, None, :]
    ).reshape(-1)
    select = (
        jnp.arange(modes_count, dtype=jnp.int32)[:, None] == mode_at[None, :]
    ).astype(jnp.float32)
    exact = functools.partial(jnp.dot, precision=lax.Precision.HIGHEST)
    part_eye = jnp.eye(2, dtype=jnp.float32)
    analysis = in_three(jnp.kron(part_eye, exact(mode_analysis, select)))
    synthesis = in_three(jnp.kron(part_eye, exact(select.T, mode_synthesis)))
    rate = mode_rate[:, None]

    even, odd = folded_products(grid_state)
    sign_own = (1 - 2 * parity).astype(jnp.float32)

    def combine(partner, own):
        return (partner.astype(jnp.float32) + sign_own * own.astype(jnp.float32)).astype(
            jnp.bfloat16
        )

    tables, incoming = [], []
    for chunk, slots in enumerate(sizes):
        size = lat_count * 2 * lev_count * slots
        at = lat_count * 2 * lev_count * firsts[chunk]
        waves = all_waves[at : at + size].reshape(lat_count, 2, -1, LANES)
        fourier, table = forward_stage(waves, even, odd, slots, lon_count)
        tables.append(table)
        mirror = swap_with(fourier, "fld", 1)
        near = [combine(mirror[dist], fourier[dist]) for dist in range(lat_count)]
        near = [swap_with(piece, "lat", dist) for dist, piece in enumerate(near)]
        far = [
            swap_with(jnp.stack([block[dist] for block in near]), "lev", dist)
            for dist in range(1, lev_count)
        ]
        incoming.append((near, far))
    hemis = []
    for chunk, slots in enumerate(sizes):
        returned = legendre_stage(
            *incoming[chunk],
            legendre,
            numbers,
            analysis,
            synthesis,
            rate,
            wave_count,
            lats_here,
            slots,
            firsts[chunk],
        )
        partner = swap_with(returned, "fld", 1)
        arrived = [
            swap_with(combine(partner[dist], returned[dist]), "lev", dist)
            for dist in range(lev_count)
        ]
        hemis.append(
            [
                swap_with(jnp.stack([block[dist] for block in arrived]), "lat", dist)
                for dist in range(lat_count)
            ]
        )
    grid_out = inverse_stage(hemis, tables)
    return grid_out.reshape(field_count, levels_here, 1, lats_here, lon_count)


def solution(mesh):
    return jax.shard_map(
        local,
        mesh=mesh,
        in_specs=(
            P("member", "lev", "fld", "lat", None),
            P(("lat", "lev"), "fld", None, None),
            P(),
            P(),
            P(),
            P(),
            P(),
        ),
        out_specs=P("member", "lev", "fld", "lat", None),
        check_vma=False,
    )
```

profile of v0, /device:TPU:0, one launch (start us, length us, event | category | flops | bytes accessed | tf_op | source)
XLA Modules:
  0.0 337.9 jit_solution(14356956472963156831)
XLA Ops:
  1.7 5.2 %shard_map.73 = (bf16[2,512,1024]{2,1,0:T(8,128)(2,1)}, bf16[2,512,1024]{2,1,0:T(8,128)(2,1)}) custom-call(bf16[2,4,1,128,2048]{4,3,2,1,0:T(8,128)(2,1)} %state.1), custom_call_target="tpu_custom_call" | custom-call | flops 8388608 | bytes 8388608 | tf_op jit(solution)/shard_map/pallas_call | solution.py:52
  7.7 4.6 %shard_map.80 = (bf16[4,4,2,16,1024]{4,3,2,1,0:T(8,128)(2,1)}, bf16[2,256,1024]{2,1,0:T(8,128)(2,1)}) custom-call(s32[4,2,32,128]{3,2,1,0:T(8,128)} %broadcast_in_dim.75.waves, bf16[1024,1024]{1,0:T(8,128)(2,1)} %bitcast.121, bf16[1024,1024]{1,0:T(8,128)(2,1)} %bitcast.125), custom_call_target="tpu_custom_call" | custom-call | flops 1073741824 | bytes 6291456 | tf_op jit(solution)/shard_map/pallas_call | solution.py:137
  13.6 4.5 %shard_map.78 = (bf16[4,4,2,16,1024]{4,3,2,1,0:T(8,128)(2,1)}, bf16[2,256,1024]{2,1,0:T(8,128)(2,1)}) custom-call(s32[4,2,32,128]{3,2,1,0:T(8,128)} %broadcast_in_dim.73.waves, bf16[1024,1024]{1,0:T(8,128)(2,1)} %bitcast.122, bf16[1024,1024]{1,0:T(8,128)(2,1)} %bitcast.126), custom_call_target="tpu_custom_call" | custom-call | flops 1073741824 | bytes 6291456 | tf_op jit(solution)/shard_map/pallas_call | solution.py:137
  19.0 4.6 %shard_map.76 = (bf16[4,4,2,16,1024]{4,3,2,1,0:T(8,128)(2,1)}, bf16[2,256,1024]{2,1,0:T(8,128)(2,1)}) custom-call(s32[4,2,32,128]{3,2,1,0:T(8,128)} %broadcast_in_dim.71.waves, bf16[1024,1024]{1,0:T(8,128)(2,1)} %bitcast.123, bf16[1024,1024]{1,0:T(8,128)(2,1)} %bitcast.127), custom_call_target="tpu_custom_call" | custom-call | flops 1073741824 | bytes 6291456 | tf_op jit(solution)/shard_map/pallas_call | solution.py:137
  24.9 4.7 %shard_map.74 = (bf16[4,4,2,16,1024]{4,3,2,1,0:T(8,128)(2,1)}, bf16[2,256,1024]{2,1,0:T(8,128)(2,1)}) custom-call(s32[4,2,32,128]{3,2,1,0:T(8,128)} %broadcast_in_dim.68.waves, bf16[1024,1024]{1,0:T(8,128)(2,1)} %bitcast.124, bf16[1024,1024]{1,0:T(8,128)(2,1)} %bitcast.128), custom_call_target="tpu_custom_call" | custom-call | flops 1073741824 | bytes 6291456 | tf_op jit(solution)/shard_map/pallas_call | solution.py:137
  36.1 5.1 %collective-permute-start.45 = (bf16[4,2,16,1024]{3,2,1,0:T(8,128)(2,1)S(1)}, bf16[4,2,16,1024]{3,2,1,0:T(8,128)(2,1)S(1)}, u32[]{:S(2)}, u32[]{:S(2)}) collective-permute-start(bf16[4,2,16,1024]{3,2,1,0:T(8,128)(2,1)S(1)} %get-tuple-element.40), channel_id=1, source_target_pairs={{0,24},{8,16},{16,8},{24,0},{1,25},{9,17},{17,9},{25,1},{2,26},{10... | collective-permute-start | bytes 786440 | tf_op jit(solution)/shard_map/ppermute | solution.py:19
  43.6 3.8 %collective-permute-start.31 = (bf16[4,2,16,1024]{3,2,1,0:T(8,128)(2,1)S(1)}, bf16[4,2,16,1024]{3,2,1,0:T(8,128)(2,1)S(1)}, u32[]{:S(2)}, u32[]{:S(2)}) collective-permute-start(bf16[4,2,16,1024]{3,2,1,0:T(8,128)(2,1)S(1)} %get-tuple-element.48), channel_id=1, source_target_pairs={{0,24},{8,16},{16,8},{24,0},{1,25},{9,17},{17,9},{25,1},{2,26},{10... | collective-permute-start | bytes 786440 | tf_op jit(solution)/shard_map/ppermute | solution.py:19
  51.0 9.3 %collective-permute-start.29 = (bf16[4,2,16,1024]{3,2,1,0:T(8,128)(2,1)S(1)}, bf16[4,2,16,1024]{3,2,1,0:T(8,128)(2,1)S(1)}, u32[]{:S(2)}, u32[]{:S(2)}) collective-permute-start(bf16[4,2,16,1024]{3,2,1,0:T(8,128)(2,1)S(1)} %get-tuple-element.50), channel_id=1, source_target_pairs={{0,8},{8,0},{16,24},{24,16},{1,9},{9,1},{17,25},{25,17},{2,10},{10... | collective-permute-start | bytes 786440 | tf_op jit(solution)/shard_map/ppermute | solution.py:19
  60.3 15.6 %collective-permute-done.44.refs_2_ = bf16[4,2,16,1024]{3,2,1,0:T(8,128)(2,1)S(1)} collective-permute-done((bf16[4,2,16,1024]{3,2,1,0:T(8,128)(2,1)S(1)}, bf16[4,2,16,1024]{3,2,1,0:T(8,128)(2,1)S(1)}, u32[]{:S(2)}, u32[]{:S(2)}) %collective-permute-start.44) | collective-permute-done | bytes 262176 | tf_op jit(solution)/shard_map/ppermute | solution.py:19
  78.6 14.7 %collective-permute-start.15 = (bf16[4,2,16,1024]{3,2,1,0:T(8,128)(2,1)S(1)}, bf16[4,2,16,1024]{3,2,1,0:T(8,128)(2,1)S(1)}, u32[]{:S(2)}, u32[]{:S(2)}) collective-permute-start(bf16[4,2,16,1024]{3,2,1,0:T(8,128)(2,1)S(1)} %get-tuple-element.58), channel_id=1, source_target_pairs={{0,8},{8,0},{16,24},{24,16},{1,9},{9,1},{17,25},{25,17},{2,10},{10... | collective-permute-start | bytes 786440 | tf_op jit(solution)/shard_map/ppermute | solution.py:19
  93.3 5.1 %collective-permute-done.30.refs_2_ = bf16[4,2,16,1024]{3,2,1,0:T(8,128)(2,1)S(1)} collective-permute-done((bf16[4,2,16,1024]{3,2,1,0:T(8,128)(2,1)S(1)}, bf16[4,2,16,1024]{3,2,1,0:T(8,128)(2,1)S(1)}, u32[]{:S(2)}, u32[]{:S(2)}) %collective-permute-start.30) | collective-permute-done | bytes 262176 | tf_op jit(solution)/shard_map/ppermute | solution.py:19
  101.1 14.7 %collective-permute-start.1 = (bf16[4,2,16,1024]{3,2,1,0:T(8,128)(2,1)S(1)}, bf16[4,2,16,1024]{3,2,1,0:T(8,128)(2,1)S(1)}, u32[]{:S(2)}, u32[]{:S(2)}) collective-permute-start(bf16[4,2,16,1024]{3,2,1,0:T(8,128)(2,1)S(1)} %get-tuple-element.66), channel_id=1, source_target_pairs={{0,8},{8,0},{16,24},{24,16},{1,9},{9,1},{17,25},{25,17},{2,10},{10... | collective-permute-start | bytes 786440 | tf_op jit(solution)/shard_map/ppermute | solution.py:19
  116.6 4.3 %collective-permute-done.16.refs_2_ = bf16[4,2,16,1024]{3,2,1,0:T(8,128)(2,1)S(1)} collective-permute-done((bf16[4,2,16,1024]{3,2,1,0:T(8,128)(2,1)S(1)}, bf16[4,2,16,1024]{3,2,1,0:T(8,128)(2,1)S(1)}, u32[]{:S(2)}, u32[]{:S(2)}) %collective-permute-start.16) | collective-permute-done | bytes 262176 | tf_op jit(solution)/shard_map/ppermute | solution.py:19
  127.4 3.8 %collective-permute-done.2.refs_2_ = bf16[4,2,16,1024]{3,2,1,0:T(8,128)(2,1)S(1)} collective-permute-done((bf16[4,2,16,1024]{3,2,1,0:T(8,128)(2,1)S(1)}, bf16[4,2,16,1024]{3,2,1,0:T(8,128)(2,1)S(1)}, u32[]{:S(2)}, u32[]{:S(2)}) %collective-permute-start.2) | collective-permute-done | bytes 262176 | tf_op jit(solution)/shard_map/ppermute | solution.py:19
  140.7 10.8 %shard_map.81 = bf16[4,4,2,16,1024]{4,3,2,1,0:T(8,128)(2,1)} custom-call(s32[98]{0:T(128)} %pad_add_fusion.2.numbers, bf16[4,2,16,1024]{3,2,1,0:T(8,128)(2,1)} %bitcast.132, bf16[4,2,16,1024]{3,2,1,0:T(8,128)(2,1)} %copy-done.23, bf16[4,2,16,1024]{3,2,1,0:T(8,128)(2,1)} %copy-done.20, bf16[4,2,16,1024]{3,2,1,0:T(8,128)(2,1)} %copy-done.19, ...), custom_call_target="tpu_custom_call" | custom-call | flops 1593835520 | bytes 7340032 | tf_op jit(solution)/shard_map/pallas_call | solution.py:354
  159.2 10.5 %shard_map.79 = bf16[4,4,2,16,1024]{4,3,2,1,0:T(8,128)(2,1)} custom-call(s32[98]{0:T(128)} %pad_add_fusion.2.numbers, bf16[4,2,16,1024]{3,2,1,0:T(8,128)(2,1)} %bitcast.131, bf16[4,2,16,1024]{3,2,1,0:T(8,128)(2,1)} %copy-done.25, bf16[4,2,16,1024]{3,2,1,0:T(8,128)(2,1)} %copy-done.18, bf16[4,2,16,1024]{3,2,1,0:T(8,128)(2,1)} %copy-done.14, ...), custom_call_target="tpu_custom_call" | custom-call | flops 1593835520 | bytes 7340032 | tf_op jit(solution)/shard_map/pallas_call | solution.py:354
  176.7 10.6 %shard_map.77 = bf16[4,4,2,16,1024]{4,3,2,1,0:T(8,128)(2,1)} custom-call(s32[98]{0:T(128)} %pad_add_fusion.2.numbers, bf16[4,2,16,1024]{3,2,1,0:T(8,128)(2,1)} %bitcast.130, bf16[4,2,16,1024]{3,2,1,0:T(8,128)(2,1)} %copy-done.22, bf16[4,2,16,1024]{3,2,1,0:T(8,128)(2,1)} %copy-done.17, bf16[4,2,16,1024]{3,2,1,0:T(8,128)(2,1)} %copy-done.15, ...), custom_call_target="tpu_custom_call" | custom-call | flops 1593835520 | bytes 7340032 | tf_op jit(solution)/shard_map/pallas_call | solution.py:354
  189.4 10.6 %shard_map.75 = bf16[4,4,2,16,1024]{4,3,2,1,0:T(8,128)(2,1)} custom-call(s32[98]{0:T(128)} %pad_add_fusion.2.numbers, bf16[4,2,16,1024]{3,2,1,0:T(8,128)(2,1)} %bitcast.129, bf16[4,2,16,1024]{3,2,1,0:T(8,128)(2,1)} %copy-done.24, bf16[4,2,16,1024]{3,2,1,0:T(8,128)(2,1)} %copy-done.21, bf16[4,2,16,1024]{3,2,1,0:T(8,128)(2,1)} %copy-done.16, ...), custom_call_target="tpu_custom_call" | custom-call | flops 1593835520 | bytes 7340032 | tf_op jit(solution)/shard_map/pallas_call | solution.py:354
  211.4 5.0 %collective-permute-done.51 = bf16[4,2,16,1024]{3,2,1,0:T(8,128)(2,1)S(1)} collective-permute-done((bf16[4,2,16,1024]{3,2,1,0:T(8,128)(2,1)S(1)}, bf16[4,2,16,1024]{3,2,1,0:T(8,128)(2,1)S(1)}, u32[]{:S(2)}, u32[]{:S(2)}) %collective-permute-start.51) | collective-permute-done | bytes 262176 | tf_op jit(solution)/shard_map/ppermute | solution.py:19
  218.6 3.4 %collective-permute-done.38 = bf16[4,2,16,1024]{3,2,1,0:T(8,128)(2,1)S(1)} collective-permute-done((bf16[4,2,16,1024]{3,2,1,0:T(8,128)(2,1)S(1)}, bf16[4,2,16,1024]{3,2,1,0:T(8,128)(2,1)S(1)}, u32[]{:S(2)}, u32[]{:S(2)}) %collective-permute-start.38) | collective-permute-done | bytes 262176 | tf_op jit(solution)/shard_map/ppermute | solution.py:19
  222.6 4.9 %collective-permute-done.37 = bf16[4,2,16,1024]{3,2,1,0:T(8,128)(2,1)S(1)} collective-permute-done((bf16[4,2,16,1024]{3,2,1,0:T(8,128)(2,1)S(1)}, bf16[4,2,16,1024]{3,2,1,0:T(8,128)(2,1)S(1)}, u32[]{:S(2)}, u32[]{:S(2)}) %collective-permute-start.37) | collective-permute-done | bytes 262176 | tf_op jit(solution)/shard_map/ppermute | solution.py:19
  229.8 3.4 %collective-permute-done.24 = bf16[4,2,16,1024]{3,2,1,0:T(8,128)(2,1)S(1)} collective-permute-done((bf16[4,2,16,1024]{3,2,1,0:T(8,128)(2,1)S(1)}, bf16[4,2,16,1024]{3,2,1,0:T(8,128)(2,1)S(1)}, u32[]{:S(2)}, u32[]{:S(2)}) %collective-permute-start.24) | collective-permute-done | bytes 262176 | tf_op jit(solution)/shard_map/ppermute | solution.py:19
  234.8 4.0 %collective-permute-done.23 = bf16[4,2,16,1024]{3,2,1,0:T(8,128)(2,1)S(1)} collective-permute-done((bf16[4,2,16,1024]{3,2,1,0:T(8,128)(2,1)S(1)}, bf16[4,2,16,1024]{3,2,1,0:T(8,128)(2,1)S(1)}, u32[]{:S(2)}, u32[]{:S(2)}) %collective-permute-start.23) | collective-permute-done | bytes 262176 | tf_op jit(solution)/shard_map/ppermute | solution.py:19
  238.9 3.0 collective-permute-start.54
  249.7 3.1 collective-permute-start.40
  254.2 6.1 %collective-permute-done.54.refs_14_ = bf16[4,2,16,1024]{3,2,1,0:T(8,128)(2,1)S(1)} collective-permute-done((bf16[4,2,16,1024]{3,2,1,0:T(8,128)(2,1)S(1)}, bf16[4,2,16,1024]{3,2,1,0:T(8,128)(2,1)S(1)}, u32[]{:S(2)}, u32[]{:S(2)}) %collective-permute-start.54) | collective-permute-done | bytes 262176 | tf_op jit(solution)/shard_map/ppermute | solution.py:19
  260.5 18.3 %collective-permute-start.26 = (bf16[4,2,16,1024]{3,2,1,0:T(8,128)(2,1)S(1)}, bf16[4,2,16,1024]{3,2,1,0:T(8,128)(2,1)S(1)}, u32[]{:S(2)}, u32[]{:S(2)}) collective-permute-start(bf16[4,2,16,1024]{3,2,1,0:T(8,128)(2,1)S(1)} %pad_maximum_fusion.12), channel_id=1, source_target_pairs={{0,16},{8,24},{16,0},{24,8},{1,17},{9,25},{17,1},{25,9},{2,18},{10... | collective-permute-start | bytes 786440 | tf_op jit(solution)/shard_map/ppermute | solution.py:19
  280.1 13.9 %collective-permute-done.40.refs_10_ = bf16[4,2,16,1024]{3,2,1,0:T(8,128)(2,1)S(1)} collective-permute-done((bf16[4,2,16,1024]{3,2,1,0:T(8,128)(2,1)S(1)}, bf16[4,2,16,1024]{3,2,1,0:T(8,128)(2,1)S(1)}, u32[]{:S(2)}, u32[]{:S(2)}) %collective-permute-start.40) | collective-permute-done | bytes 262176 | tf_op jit(solution)/shard_map/ppermute | solution.py:19
  294.1 7.2 %collective-permute-start.12 = (bf16[4,2,16,1024]{3,2,1,0:T(8,128)(2,1)S(1)}, bf16[4,2,16,1024]{3,2,1,0:T(8,128)(2,1)S(1)}, u32[]{:S(2)}, u32[]{:S(2)}) collective-permute-start(bf16[4,2,16,1024]{3,2,1,0:T(8,128)(2,1)S(1)} %pad_maximum_fusion.5), channel_id=1, source_target_pairs={{0,16},{8,24},{16,0},{24,8},{1,17},{9,25},{17,1},{25,9},{2,18},{10... | collective-permute-start | bytes 786440 | tf_op jit(solution)/shard_map/ppermute | solution.py:19
  304.9 11.7 %collective-permute-done.26.refs_6_ = bf16[4,2,16,1024]{3,2,1,0:T(8,128)(2,1)S(1)} collective-permute-done((bf16[4,2,16,1024]{3,2,1,0:T(8,128)(2,1)S(1)}, bf16[4,2,16,1024]{3,2,1,0:T(8,128)(2,1)S(1)}, u32[]{:S(2)}, u32[]{:S(2)}) %collective-permute-start.26) | collective-permute-done | bytes 262176 | tf_op jit(solution)/shard_map/ppermute | solution.py:19
  316.6 11.2 %collective-permute-done.12.refs_2_ = bf16[4,2,16,1024]{3,2,1,0:T(8,128)(2,1)S(1)} collective-permute-done((bf16[4,2,16,1024]{3,2,1,0:T(8,128)(2,1)S(1)}, bf16[4,2,16,1024]{3,2,1,0:T(8,128)(2,1)S(1)}, u32[]{:S(2)}, u32[]{:S(2)}) %collective-permute-start.12) | collective-permute-done | bytes 262176 | tf_op jit(solution)/shard_map/ppermute | solution.py:19
  328.6 9.1 %shard_map.82 = bf16[1024,2048]{1,0:T(8,128)(2,1)} custom-call(bf16[4,2,16,1024]{3,2,1,0:T(8,128)(2,1)} %pad_maximum_fusion.3.refs_0_, bf16[4,2,16,1024]{3,2,1,0:T(8,128)(2,1)} %copy-done.53, bf16[4,2,16,1024]{3,2,1,0:T(8,128)(2,1)} %copy-done.54, bf16[4,2,16,1024]{3,2,1,0:T(8,128)(2,1)} %copy-done.55, bf16[4,2,16,1024]{3,2,1,0:T(8,128)(2,1)} %pad_maximum_fusion.10.refs_4_, ...), custom_call_target="tpu_custom_call" | custom-call | flops 4294967296 | bytes 12582912 | tf_op jit(solution)/shard_map/pallas_call | solution.py:190
  (311 shorter events, 90.1 us)
Async XLA Ops:
  12.2 22.2 %collective-permute-start.42 = (bf16[4,4,2,16,1024]{4,3,2,1,0:T(8,128)(2,1)}, bf16[4,4,2,16,1024]{4,3,2,1,0:T(8,128)(2,1)}, u32[]{:S(2)}, u32[]{:S(2)}) collective-permute-start(bf16[4,4,2,16,1024]{4,3,2,1,0:T(8,128)(2,1)} %get-tuple-element.20), channel_id=1, source_target_pairs={{0,1},{1,0},{2,3},{3,2},{4,5},{5,4},{6,7},{7,6},{8,9},{9,8},{10,11... | collective-permute-start | bytes 3145736 | tf_op jit(solution)/shard_map/ppermute | solution.py:19
  18.1 23.1 %collective-permute-start.28 = (bf16[4,4,2,16,1024]{4,3,2,1,0:T(8,128)(2,1)}, bf16[4,4,2,16,1024]{4,3,2,1,0:T(8,128)(2,1)}, u32[]{:S(2)}, u32[]{:S(2)}) collective-permute-start(bf16[4,4,2,16,1024]{4,3,2,1,0:T(8,128)(2,1)} %get-tuple-element.19), channel_id=1, source_target_pairs={{0,1},{1,0},{2,3},{3,2},{4,5},{5,4},{6,7},{7,6},{8,9},{9,8},{10,11... | collective-permute-start | bytes 3145736 | tf_op jit(solution)/shard_map/ppermute | solution.py:19
  23.5 20.0 %collective-permute-start.14 = (bf16[4,4,2,16,1024]{4,3,2,1,0:T(8,128)(2,1)}, bf16[4,4,2,16,1024]{4,3,2,1,0:T(8,128)(2,1)S(1)}, u32[]{:S(2)}, u32[]{:S(2)}) collective-permute-start(bf16[4,4,2,16,1024]{4,3,2,1,0:T(8,128)(2,1)} %get-tuple-element.18), channel_id=1, source_target_pairs={{0,1},{1,0},{2,3},{3,2},{4,5},{5,4},{6,7},{7,6},{8,9},{9,8},{10,11... | collective-permute-start | bytes 3145736 | tf_op jit(solution)/shard_map/ppermute | solution.py:19
  41.2 34.7 %collective-permute-start.44 = (bf16[4,2,16,1024]{3,2,1,0:T(8,128)(2,1)S(1)}, bf16[4,2,16,1024]{3,2,1,0:T(8,128)(2,1)S(1)}, u32[]{:S(2)}, u32[]{:S(2)}) collective-permute-start(bf16[4,2,16,1024]{3,2,1,0:T(8,128)(2,1)S(1)} %get-tuple-element.41), channel_id=1, source_target_pairs={{0,16},{8,24},{16,0},{24,8},{1,17},{9,25},{17,1},{25,9},{2,18},{10... | collective-permute-start | bytes 786440 | tf_op jit(solution)/shard_map/ppermute | solution.py:19
  41.2 37.2 %collective-permute-start.43 = (bf16[4,2,16,1024]{3,2,1,0:T(8,128)(2,1)S(1)}, bf16[4,2,16,1024]{3,2,1,0:T(8,128)(2,1)S(1)}, u32[]{:S(2)}, u32[]{:S(2)}) collective-permute-start(bf16[4,2,16,1024]{3,2,1,0:T(8,128)(2,1)S(1)} %get-tuple-element.42), channel_id=1, source_target_pairs={{0,8},{8,0},{16,24},{24,16},{1,9},{9,1},{17,25},{25,17},{2,10},{10... | collective-permute-start | bytes 786440 | tf_op jit(solution)/shard_map/ppermute | solution.py:19
  43.6 35.0 %collective-permute-start.31 = (bf16[4,2,16,1024]{3,2,1,0:T(8,128)(2,1)S(1)}, bf16[4,2,16,1024]{3,2,1,0:T(8,128)(2,1)S(1)}, u32[]{:S(2)}, u32[]{:S(2)}) collective-permute-start(bf16[4,2,16,1024]{3,2,1,0:T(8,128)(2,1)S(1)} %get-tuple-element.48), channel_id=1, source_target_pairs={{0,24},{8,16},{16,8},{24,0},{1,25},{9,17},{17,9},{25,1},{2,26},{10... | collective-permute-start | bytes 786440 | tf_op jit(solution)/shard_map/ppermute | solution.py:19
  47.8 50.5 %collective-permute-start.30 = (bf16[4,2,16,1024]{3,2,1,0:T(8,128)(2,1)S(1)}, bf16[4,2,16,1024]{3,2,1,0:T(8,128)(2,1)S(1)}, u32[]{:S(2)}, u32[]{:S(2)}) collective-permute-start(bf16[4,2,16,1024]{3,2,1,0:T(8,128)(2,1)S(1)} %get-tuple-element.49), channel_id=1, source_target_pairs={{0,16},{8,24},{16,0},{24,8},{1,17},{9,25},{17,1},{25,9},{2,18},{10... | collective-permute-start | bytes 786440 | tf_op jit(solution)/shard_map/ppermute | solution.py:19
  51.0 50.0 %collective-permute-start.29 = (bf16[4,2,16,1024]{3,2,1,0:T(8,128)(2,1)S(1)}, bf16[4,2,16,1024]{3,2,1,0:T(8,128)(2,1)S(1)}, u32[]{:S(2)}, u32[]{:S(2)}) collective-permute-start(bf16[4,2,16,1024]{3,2,1,0:T(8,128)(2,1)S(1)} %get-tuple-element.50), channel_id=1, source_target_pairs={{0,8},{8,0},{16,24},{24,16},{1,9},{9,1},{17,25},{25,17},{2,10},{10... | collective-permute-start | bytes 786440 | tf_op jit(solution)/shard_map/ppermute | solution.py:19
  75.9 25.2 %collective-permute-start.17 = (bf16[4,2,16,1024]{3,2,1,0:T(8,128)(2,1)S(1)}, bf16[4,2,16,1024]{3,2,1,0:T(8,128)(2,1)S(1)}, u32[]{:S(2)}, u32[]{:S(2)}) collective-permute-start(bf16[4,2,16,1024]{3,2,1,0:T(8,128)(2,1)S(1)} %get-tuple-element.56), channel_id=1, source_target_pairs={{0,24},{8,16},{16,8},{24,0},{1,25},{9,17},{17,9},{25,1},{2,26},{10... | collective-permute-start | bytes 786440 | tf_op jit(solution)/shard_map/ppermute | solution.py:19
  78.4 42.5 %collective-permute-start.16 = (bf16[4,2,16,1024]{3,2,1,0:T(8,128)(2,1)S(1)}, bf16[4,2,16,1024]{3,2,1,0:T(8,128)(2,1)S(1)}, u32[]{:S(2)}, u32[]{:S(2)}) collective-permute-start(bf16[4,2,16,1024]{3,2,1,0:T(8,128)(2,1)S(1)} %get-tuple-element.57), channel_id=1, source_target_pairs={{0,16},{8,24},{16,0},{24,8},{1,17},{9,25},{17,1},{25,9},{2,18},{10... | collective-permute-start | bytes 786440 | tf_op jit(solution)/shard_map/ppermute | solution.py:19
  78.6 44.5 %collective-permute-start.15 = (bf16[4,2,16,1024]{3,2,1,0:T(8,128)(2,1)S(1)}, bf16[4,2,16,1024]{3,2,1,0:T(8,128)(2,1)S(1)}, u32[]{:S(2)}, u32[]{:S(2)}) collective-permute-start(bf16[4,2,16,1024]{3,2,1,0:T(8,128)(2,1)S(1)} %get-tuple-element.58), channel_id=1, source_target_pairs={{0,8},{8,0},{16,24},{24,16},{1,9},{9,1},{17,25},{25,17},{2,10},{10... | collective-permute-start | bytes 786440 | tf_op jit(solution)/shard_map/ppermute | solution.py:19
  98.4 27.7 %collective-permute-start.3 = (bf16[4,2,16,1024]{3,2,1,0:T(8,128)(2,1)S(1)}, bf16[4,2,16,1024]{3,2,1,0:T(8,128)(2,1)S(1)}, u32[]{:S(2)}, u32[]{:S(2)}) collective-permute-start(bf16[4,2,16,1024]{3,2,1,0:T(8,128)(2,1)S(1)} %get-tuple-element.64), channel_id=1, source_target_pairs={{0,24},{8,16},{16,8},{24,0},{1,25},{9,17},{17,9},{25,1},{2,26},{10... | collective-permute-start | bytes 786440 | tf_op jit(solution)/shard_map/ppermute | solution.py:19
  100.9 30.2 %collective-permute-start.2 = (bf16[4,2,16,1024]{3,2,1,0:T(8,128)(2,1)S(1)}, bf16[4,2,16,1024]{3,2,1,0:T(8,128)(2,1)S(1)}, u32[]{:S(2)}, u32[]{:S(2)}) collective-permute-start(bf16[4,2,16,1024]{3,2,1,0:T(8,128)(2,1)S(1)} %get-tuple-element.65), channel_id=1, source_target_pairs={{0,16},{8,24},{16,0},{24,8},{1,17},{9,25},{17,1},{25,9},{2,18},{10... | collective-permute-start | bytes 786440 | tf_op jit(solution)/shard_map/ppermute | solution.py:19
  101.1 34.5 %collective-permute-start.1 = (bf16[4,2,16,1024]{3,2,1,0:T(8,128)(2,1)S(1)}, bf16[4,2,16,1024]{3,2,1,0:T(8,128)(2,1)S(1)}, u32[]{:S(2)}, u32[]{:S(2)}) collective-permute-start(bf16[4,2,16,1024]{3,2,1,0:T(8,128)(2,1)S(1)} %get-tuple-element.66), channel_id=1, source_target_pairs={{0,8},{8,0},{16,24},{24,16},{1,9},{9,1},{17,25},{25,17},{2,10},{10... | collective-permute-start | bytes 786440 | tf_op jit(solution)/shard_map/ppermute | solution.py:19
  131.2 25.3 %collective-permute-start.32 = (bf16[4,2,16,1024]{3,2,1,0:T(8,128)(2,1)}, bf16[4,2,16,1024]{3,2,1,0:T(8,128)(2,1)S(1)}, u32[]{:S(2)}, u32[]{:S(2)}) collective-permute-start(bf16[4,2,16,1024]{3,2,1,0:T(8,128)(2,1)} %pad_maximum_fusion.14), channel_id=1, source_target_pairs={{0,2},{2,0},{4,6},{6,4},{1,3},{3,1},{5,7},{7,5},{8,10},{10,8},{12,... | collective-permute-start | bytes 786440 | tf_op jit(solution)/shard_map/ppermute | solution.py:19
  135.6 22.4 %collective-permute-start.33 = (bf16[4,2,16,1024]{3,2,1,0:T(8,128)(2,1)}, bf16[4,2,16,1024]{3,2,1,0:T(8,128)(2,1)S(1)}, u32[]{:S(2)}, u32[]{:S(2)}) collective-permute-start(bf16[4,2,16,1024]{3,2,1,0:T(8,128)(2,1)} %pad_maximum_fusion.15), channel_id=1, source_target_pairs={{0,4},{2,6},{4,0},{6,2},{1,5},{3,7},{5,1},{7,3},{8,12},{10,14},{12... | collective-permute-start | bytes 786440 | tf_op jit(solution)/shard_map/ppermute | solution.py:19
  137.9 20.6 %collective-permute-start.34 = (bf16[4,2,16,1024]{3,2,1,0:T(8,128)(2,1)}, bf16[4,2,16,1024]{3,2,1,0:T(8,128)(2,1)S(1)}, u32[]{:S(2)}, u32[]{:S(2)}) collective-permute-start(bf16[4,2,16,1024]{3,2,1,0:T(8,128)(2,1)} %pad_maximum_fusion.16), channel_id=1, source_target_pairs={{0,6},{2,4},{4,2},{6,0},{1,7},{3,5},{5,3},{7,1},{8,14},{10,12},{12... | collective-permute-start | bytes 786440 | tf_op jit(solution)/shard_map/ppermute | solution.py:19
  138.4 34.5 %collective-permute-start.18 = (bf16[4,2,16,1024]{3,2,1,0:T(8,128)(2,1)}, bf16[4,2,16,1024]{3,2,1,0:T(8,128)(2,1)S(1)}, u32[]{:S(2)}, u32[]{:S(2)}) collective-permute-start(bf16[4,2,16,1024]{3,2,1,0:T(8,128)(2,1)} %pad_maximum_fusion.7), channel_id=1, source_target_pairs={{0,2},{2,0},{4,6},{6,4},{1,3},{3,1},{5,7},{7,5},{8,10},{10,8},{12,... | collective-permute-start | bytes 786440 | tf_op jit(solution)/shard_map/ppermute | solution.py:19
  151.5 48.6 %collective-permute-start.49 = (bf16[4,4,2,16,1024]{4,3,2,1,0:T(8,128)(2,1)}, bf16[4,4,2,16,1024]{4,3,2,1,0:T(8,128)(2,1)S(1)}, u32[]{:S(2)}, u32[]{:S(2)}) collective-permute-start(bf16[4,4,2,16,1024]{4,3,2,1,0:T(8,128)(2,1)} %shard_map.81), channel_id=1, source_target_pairs={{0,1},{1,0},{2,3},{3,2},{4,5},{5,4},{6,7},{7,6},{8,9},{9,8},{10,11... | collective-permute-start | bytes 3145736 | tf_op jit(solution)/shard_map/ppermute | solution.py:19
  169.7 33.0 %collective-permute-start.35 = (bf16[4,4,2,16,1024]{4,3,2,1,0:T(8,128)(2,1)}, bf16[4,4,2,16,1024]{4,3,2,1,0:T(8,128)(2,1)S(1)}, u32[]{:S(2)}, u32[]{:S(2)}) collective-permute-start(bf16[4,4,2,16,1024]{4,3,2,1,0:T(8,128)(2,1)} %shard_map.79), channel_id=1, source_target_pairs={{0,1},{1,0},{2,3},{3,2},{4,5},{5,4},{6,7},{7,6},{8,9},{9,8},{10,11... | collective-permute-start | bytes 3145736 | tf_op jit(solution)/shard_map/ppermute | solution.py:19
  217.9 20.9 %collective-permute-start.23 = (bf16[4,2,16,1024]{3,2,1,0:T(8,128)(2,1)S(1)}, bf16[4,2,16,1024]{3,2,1,0:T(8,128)(2,1)S(1)}, u32[]{:S(2)}, u32[]{:S(2)}) collective-permute-start(bf16[4,2,16,1024]{3,2,1,0:T(8,128)(2,1)S(1)} %get-tuple-element.54), channel_id=1, source_target_pairs={{0,4},{2,6},{4,0},{6,2},{1,5},{3,7},{5,1},{7,3},{8,12},{10,14},{12... | collective-permute-start | bytes 786440 | tf_op jit(solution)/shard_map/ppermute | solution.py:19
  229.1 20.4 %collective-permute-start.9 = (bf16[4,2,16,1024]{3,2,1,0:T(8,128)(2,1)S(1)}, bf16[4,2,16,1024]{3,2,1,0:T(8,128)(2,1)S(1)}, u32[]{:S(2)}, u32[]{:S(2)}) collective-permute-start(bf16[4,2,16,1024]{3,2,1,0:T(8,128)(2,1)S(1)} %get-tuple-element.62), channel_id=1, source_target_pairs={{0,4},{2,6},{4,0},{6,2},{1,5},{3,7},{5,1},{7,3},{8,12},{10,14},{12... | collective-permute-start | bytes 786440 | tf_op jit(solution)/shard_map/ppermute | solution.py:19
  238.9 21.4 %collective-permute-start.54 = (bf16[4,2,16,1024]{3,2,1,0:T(8,128)(2,1)S(1)}, bf16[4,2,16,1024]{3,2,1,0:T(8,128)(2,1)S(1)}, u32[]{:S(2)}, u32[]{:S(2)}) collective-permute-start(bf16[4,2,16,1024]{3,2,1,0:T(8,128)(2,1)S(1)} %pad_maximum_fusion.26), channel_id=1, source_target_pairs={{0,16},{8,24},{16,0},{24,8},{1,17},{9,25},{17,1},{25,9},{2,18},{10... | collective-permute-start | bytes 786440 | tf_op jit(solution)/shard_map/ppermute | solution.py:19
  249.5 29.3 %collective-permute-start.39 = (bf16[4,2,16,1024]{3,2,1,0:T(8,128)(2,1)S(1)}, bf16[4,2,16,1024]{3,2,1,0:T(8,128)(2,1)S(1)}, u32[]{:S(2)}, u32[]{:S(2)}) collective-permute-start(bf16[4,2,16,1024]{3,2,1,0:T(8,128)(2,1)S(1)} %pad_maximum_fusion.18), channel_id=1, source_target_pairs={{0,8},{8,0},{16,24},{24,16},{1,9},{9,1},{17,25},{25,17},{2,10},{10... | collective-permute-start | bytes 786440 | tf_op jit(solution)/shard_map/ppermute | solution.py:19
  249.7 44.3 %collective-permute-start.40 = (bf16[4,2,16,1024]{3,2,1,0:T(8,128)(2,1)S(1)}, bf16[4,2,16,1024]{3,2,1,0:T(8,128)(2,1)S(1)}, u32[]{:S(2)}, u32[]{:S(2)}) collective-permute-start(bf16[4,2,16,1024]{3,2,1,0:T(8,128)(2,1)S(1)} %pad_maximum_fusion.19), channel_id=1, source_target_pairs={{0,16},{8,24},{16,0},{24,8},{1,17},{9,25},{17,1},{25,9},{2,18},{10... | collective-permute-start | bytes 786440 | tf_op jit(solution)/shard_map/ppermute | solution.py:19
  252.8 41.2 %collective-permute-start.41 = (bf16[4,2,16,1024]{3,2,1,0:T(8,128)(2,1)S(1)}, bf16[4,2,16,1024]{3,2,1,0:T(8,128)(2,1)S(1)}, u32[]{:S(2)}, u32[]{:S(2)}) collective-permute-start(bf16[4,2,16,1024]{3,2,1,0:T(8,128)(2,1)S(1)} %pad_maximum_fusion.20), channel_id=1, source_target_pairs={{0,24},{8,16},{16,8},{24,0},{1,25},{9,17},{17,9},{25,1},{2,26},{10... | collective-permute-start | bytes 786440 | tf_op jit(solution)/shard_map/ppermute | solution.py:19
  260.4 40.9 %collective-permute-start.25 = (bf16[4,2,16,1024]{3,2,1,0:T(8,128)(2,1)S(1)}, bf16[4,2,16,1024]{3,2,1,0:T(8,128)(2,1)S(1)}, u32[]{:S(2)}, u32[]{:S(2)}) collective-permute-start(bf16[4,2,16,1024]{3,2,1,0:T(8,128)(2,1)S(1)} %pad_maximum_fusion.11), channel_id=1, source_target_pairs={{0,8},{8,0},{16,24},{24,16},{1,9},{9,1},{17,25},{25,17},{2,10},{10... | collective-permute-start | bytes 786440 | tf_op jit(solution)/shard_map/ppermute | solution.py:19
  260.5 56.1 %collective-permute-start.26 = (bf16[4,2,16,1024]{3,2,1,0:T(8,128)(2,1)S(1)}, bf16[4,2,16,1024]{3,2,1,0:T(8,128)(2,1)S(1)}, u32[]{:S(2)}, u32[]{:S(2)}) collective-permute-start(bf16[4,2,16,1024]{3,2,1,0:T(8,128)(2,1)S(1)} %pad_maximum_fusion.12), channel_id=1, source_target_pairs={{0,16},{8,24},{16,0},{24,8},{1,17},{9,25},{17,1},{25,9},{2,18},{10... | collective-permute-start | bytes 786440 | tf_op jit(solution)/shard_map/ppermute | solution.py:19
  278.8 37.8 %collective-permute-start.27 = (bf16[4,2,16,1024]{3,2,1,0:T(8,128)(2,1)S(1)}, bf16[4,2,16,1024]{3,2,1,0:T(8,128)(2,1)S(1)}, u32[]{:S(2)}, u32[]{:S(2)}) collective-permute-start(bf16[4,2,16,1024]{3,2,1,0:T(8,128)(2,1)S(1)} %pad_maximum_fusion.13), channel_id=1, source_target_pairs={{0,24},{8,16},{16,8},{24,0},{1,25},{9,17},{17,9},{25,1},{2,26},{10... | collective-permute-start | bytes 786440 | tf_op jit(solution)/shard_map/ppermute | solution.py:19
  294.1 22.5 %collective-permute-start.11 = (bf16[4,2,16,1024]{3,2,1,0:T(8,128)(2,1)S(1)}, bf16[4,2,16,1024]{3,2,1,0:T(8,128)(2,1)S(1)}, u32[]{:S(2)}, u32[]{:S(2)}) collective-permute-start(bf16[4,2,16,1024]{3,2,1,0:T(8,128)(2,1)S(1)} %pad_maximum_fusion.4), channel_id=1, source_target_pairs={{0,8},{8,0},{16,24},{24,16},{1,9},{9,1},{17,25},{25,17},{2,10},{10... | collective-permute-start | bytes 786440 | tf_op jit(solution)/shard_map/ppermute | solution.py:19
  294.1 33.7 %collective-permute-start.12 = (bf16[4,2,16,1024]{3,2,1,0:T(8,128)(2,1)S(1)}, bf16[4,2,16,1024]{3,2,1,0:T(8,128)(2,1)S(1)}, u32[]{:S(2)}, u32[]{:S(2)}) collective-permute-start(bf16[4,2,16,1024]{3,2,1,0:T(8,128)(2,1)S(1)} %pad_maximum_fusion.5), channel_id=1, source_target_pairs={{0,16},{8,24},{16,0},{24,8},{1,17},{9,25},{17,1},{25,9},{2,18},{10... | collective-permute-start | bytes 786440 | tf_op jit(solution)/shard_map/ppermute | solution.py:19
  301.2 26.6 %collective-permute-start.13 = (bf16[4,2,16,1024]{3,2,1,0:T(8,128)(2,1)S(1)}, bf16[4,2,16,1024]{3,2,1,0:T(8,128)(2,1)S(1)}, u32[]{:S(2)}, u32[]{:S(2)}) collective-permute-start(bf16[4,2,16,1024]{3,2,1,0:T(8,128)(2,1)S(1)} %pad_maximum_fusion.6), channel_id=1, source_target_pairs={{0,24},{8,16},{16,8},{24,0},{1,25},{9,17},{17,9},{25,1},{2,26},{10... | collective-permute-start | bytes 786440 | tf_op jit(solution)/shard_map/ppermute | solution.py:19
  (80 other events, 1434.7 us)
where the time goes:
time: 341 us; the launch traced here: 338 us
  starting transfers between devices  119 us (35%)
  waiting for transfers between devices  101 us (30%)
  Pallas kernels  75.1 us (22%)
  other arithmetic  27.3 us (8%)
  local copies, waits for them, and re-layouts  13.9 us (4%)
    ppermute x56, starting transfers between devices, swap_with(): return lax.ppermute(value, axis, pairs)  119 us
    ppermute x56, waiting for transfers between devices, swap_with(): return lax.ppermute(value, axis, pairs)  101 us
    pallas_call x4, Pallas kernels, legendre_stage(): pl.pallas_call(functools.partial(legendre_kernel, lats=lats, dists=dists,...  42.4 us
    pallas_call x4, Pallas kernels, forward_stage(): pl.pallas_call(functools.partial(forward_kernel, slots=slots, lon_count=l...  18.3 us
    another operation x12, other arithmetic, local(): jnp.stack([block[dist] for block in near])  11.2 us
    pallas_call x1, Pallas kernels, inverse_stage(): pl.pallas_call(functools.partial(inverse_kernel, dists=dists, chunks=len(...  9.15 us
    convert_element_type x8, other arithmetic, combine(): (partner.astype(jnp.float32) + sign_own * own.astype(jnp.float32)).astype...  8.07 us
  transfers between devices with their start and end apart: 56, of which 19 were waited for; matrix products, arithmetic and copies ran while one was open for 11% of the time, Pallas kernels for 17%

commit v1 on v0

--- a/solution.py
+++ b/solution.py
@@ -10,13 +10,15 @@
 
 
 LANES = 128
-
-
-def swap_with(value, axis, mask):
+VMEM_LIMIT = 16 << 20
+
+
+def swap_with(value, axis, mask, near=True):
     if mask == 0:
         return value
     pairs = [(source, source ^ mask) for source in range(lax.axis_size(axis))]
-    return lax.ppermute(value, axis, pairs)
+    value = lax.ppermute(value, axis, pairs)
+    return pltpu.with_memory_space_constraint(value, pltpu.VMEM) if near else value
 
 
 def pick(table, index):
@@ -24,41 +26,58 @@
     return jnp.sum(jnp.where(index[:, None] == places[None, :], table[None, :], 0), axis=1)
 
 
-def fold_kernel(state, even, odd):
+def fold_kernel(sign, own, mirror, even, odd):
     half = even.shape[2]
     lats = even.shape[1]
     step = 16 if lats % 16 == 0 else lats
 
-    def products(rows, columns):
+    def products(state, rows, columns):
         wind_part, heat_part = state[0, 0, 0, rows, columns], state[1, 0, 0, rows, columns]
         wind, heat = wind_part.astype(jnp.float32), heat_part.astype(jnp.float32)
         return wind_part * heat_part, (wind * wind - heat * heat).astype(jnp.bfloat16)
 
+    sign_own = sign[0].astype(jnp.float32).astype(jnp.bfloat16)
     for top in range(0, lats, step):
         rows = slice(top, top + step)
         for left in range(0, half, LANES):
             columns = slice(left, left + LANES)
-            lows = products(rows, columns)
-            highs = products(rows, slice(half + left, half + left + LANES))
-            for field, (low, high) in enumerate(zip(lows, highs)):
-                even[field, rows, columns] = low + high
-                odd[field, rows, columns] = low - high
-
-
-def folded_products(grid_state):
+            pieces = [
+                [
+                    (
+                        products(mirror, rows, there),
+                        [value * sign_own for value in products(own, rows, there)],
+                    )
+                    for there in (columns, slice(half + left, half + left + LANES))
+                ]
+            ][0]
+            for field in range(2):
+                low, high = [
+                    there[field].astype(jnp.float32) + here[field].astype(jnp.float32)
+                    for there, here in pieces
+                ]
+                even[field, rows, columns] = (low + high).astype(even.dtype)
+                odd[field, rows, columns] = (low - high).astype(odd.dtype)
+
+
+def folded_products(grid_state, mirror, sign_own):
     fields, levels, _, lats, lon_count = grid_state.shape
     half = lon_count // 2
     out = jax.ShapeDtypeStruct((fields, levels * lats, half), jnp.bfloat16)
+    state = pl.BlockSpec((fields, 1, 1, lats, lon_count), lambda i, n: (0, i, 0, 0, 0))
     even, odd = pl.pallas_call(
         fold_kernel,
-        grid=(levels,),
-        in_specs=[pl.BlockSpec((fields, 1, 1, lats, lon_count), lambda i: (0, i, 0, 0, 0))],
-        out_specs=[pl.BlockSpec((fields, lats, half), lambda i: (0, i, 0))] * 2,
+        grid_spec=pltpu.PrefetchScalarGridSpec(
+            num_scalar_prefetch=1,
+            grid=(levels,),
+            in_specs=[state] * 2,
+            out_specs=[pl.BlockSpec((fields, lats, half), lambda i, n: (0, i, 0))] * 2,
+        ),
         out_shape=[out, out],
+        compiler_params=pltpu.CompilerParams(vmem_limit_bytes=VMEM_LIMIT),
         cost_estimate=pl.CostEstimate(
-            flops=grid_state.size * 4, bytes_accessed=grid_state.size * 4, transcendentals=0
-        ),
-    )(grid_state)
+            flops=grid_state.size * 8, bytes_accessed=grid_state.size * 6, transcendentals=0
+        ),
+    )(sign_own[None], grid_state, mirror)
     return even.reshape(-1, half), odd.reshape(-1, half)
 
 
@@ -85,8 +104,10 @@
     return real, imaginary
 
 
-def forward_kernel(waves, even, odd, fourier, table, *, slots, lon_count):
-    dists, levs, parities, tall, _ = fourier.shape
+def forward_kernel(waves, even, odd, *outs, slots, lon_count):
+    fourier, table = outs[:-1], outs[-1]
+    dists = len(fourier)
+    levs, parities, tall, _ = fourier[0].shape
     half = even.shape[1]
     scaling = 1.0 / math.sqrt(lon_count)
 
@@ -95,7 +116,7 @@
         fine = lax.broadcasted_iota(jnp.int32, (1, LANES), 1)
         for parity in range(parities):
             for dist in range(dists):
-                wave = waves[dist, parity]
+                wave = waves[0, dist, parity]
                 c_step, s_step = cos_sin((wave * LANES) & (lon_count - 1), lon_count // 4)
                 c_here, s_here = cos_sin((wave * fine) & (lon_count - 1), lon_count // 4)
                 c_here, s_here = c_here * scaling, s_here * scaling
@@ -119,87 +140,139 @@
             grid_rows[...],
             (((1,), (1,)), ((), ())),
             preferred_element_type=jnp.float32,
-        ).astype(fourier.dtype)
+        ).astype(table.dtype)
         for dist in range(dists):
             for lev in range(levs):
                 top = (dist * levs + lev) * tall
-                fourier[dist, lev, parity] = sums[top : top + tall]
-
-
-def forward_stage(waves, even, odd, slots, lon_count):
-    dists, parities, lines, _ = waves.shape
+                fourier[dist][lev, parity] = sums[top : top + tall]
+
+
+def forward_stage(waves, chunk, even, odd, slots, lon_count):
+    _, dists, parities, lines, _ = waves.shape
     levs = lines // slots
     rows, half = even.shape
     block = min(rows, 512)
     whole = lambda shape: pl.BlockSpec(shape, lambda i: (0,) * len(shape))
-    shape = (dists, levs, parities, 2 * slots, rows)
+    shape = (levs, parities, 2 * slots, rows)
     table_shape = (parities, dists * levs * 2 * slots, half)
     return pl.pallas_call(
         functools.partial(forward_kernel, slots=slots, lon_count=lon_count),
         grid=(rows // block,),
-        in_specs=[whole(waves.shape)] + [pl.BlockSpec((block, half), lambda i: (i, 0))] * 2,
-        out_specs=[
-            pl.BlockSpec(shape[:-1] + (block,), lambda i: (0, 0, 0, 0, i)),
-            whole(table_shape),
-        ],
-        out_shape=[
-            jax.ShapeDtypeStruct(shape, jnp.bfloat16),
-            jax.ShapeDtypeStruct(table_shape, jnp.bfloat16),
-        ],
+        in_specs=[pl.BlockSpec((1,) + waves.shape[1:], lambda i: (chunk, 0, 0, 0, 0))]
+        + [pl.BlockSpec((block, half), lambda i: (i, 0))] * 2,
+        out_specs=[pl.BlockSpec(shape[:-1] + (block,), lambda i: (0, 0, 0, i))] * dists
+        + [whole(table_shape)],
+        out_shape=[jax.ShapeDtypeStruct(shape, jnp.bfloat16)] * dists
+        + [pltpu.HBM(table_shape, jnp.bfloat16)],
+        compiler_params=pltpu.CompilerParams(vmem_limit_bytes=VMEM_LIMIT),
         cost_estimate=pl.CostEstimate(
-            flops=2 * math.prod(shape) * half,
-            bytes_accessed=4 * rows * half + 2 * math.prod(shape) + 2 * math.prod(table_shape),
+            flops=2 * dists * math.prod(shape) * half,
+            bytes_accessed=4 * rows * half + 4 * math.prod(table_shape),
             transcendentals=0,
         ),
     )(waves, even, odd)
 
 
-def inverse_kernel(*refs, dists, chunks):
-    hemis, tables, out = refs[: dists * chunks], refs[dists * chunks : -1], refs[-1]
+def inverse_kernel(*refs, levs, dists, chunks, first, last):
+    count = levs + dists - 1
+    hemis, rest = refs[: count * chunks], refs[count * chunks :]
+    tables, before, out = rest[:chunks], rest[chunks:-1], rest[-1]
     half = tables[0].shape[2]
     sums = []
     for parity in range(2):
-        total = None
+        total = None if first else before[0][parity]
         for chunk in range(chunks):
+            pieces = hemis[chunk * count : (chunk + 1) * count]
             hemi = jnp.concatenate(
-                [
-                    hemis[chunk * dists + dist][lev, parity]
-                    for dist in range(dists)
-                    for lev in range(hemis[0].shape[0])
-                ],
+                [piece[0, parity] for piece in pieces[:levs]]
+                + [piece[lev, parity] for piece in pieces[levs:] for lev in range(levs)],
                 axis=0,
             )
-            table = tables[chunk][parity]
             part = lax.dot_general(
-                hemi, table, (((0,), (0,)), ((), ())), preferred_element_type=jnp.float32
+                hemi,
+                tables[chunk][parity],
+                (((0,), (0,)), ((), ())),
+                preferred_element_type=jnp.float32,
             )
             total = part if total is None else total + part
         sums.append(total)
-    out[:, :half] = (sums[0] + sums[1]).astype(out.dtype)
-    out[:, half:] = (sums[0] - sums[1]).astype(out.dtype)
-
-
-def inverse_stage(hemis, tables):
-    rows = hemis[0][0].shape[-1]
+    if last:
+        out[:, :half] = (sums[0] + sums[1]).astype(out.dtype)
+        out[:, half:] = (sums[0] - sums[1]).astype(out.dtype)
+    else:
+        out[0], out[1] = sums
+
+
+def inverse_stage(hemis, tables, before, last):
+    rows = hemis[0][0][0].shape[-1]
     half = tables[0].shape[-1]
-    dists = len(hemis[0])
+    levs, dists = len(hemis[0][0]), len(hemis[0][1]) + 1
     block = min(rows, 256)
-    flat = [piece for pieces in hemis for piece in pieces]
+    flat, specs = [], []
+    for near, far in hemis:
+        flat += near + far
+        at = lambda i: (0, 0, 0, i)
+        specs += [pl.BlockSpec((1,) + piece.shape[1:3] + (block,), at) for piece in near]
+        specs += [pl.BlockSpec(piece.shape[:3] + (block,), at) for piece in far]
     whole = lambda shape: pl.BlockSpec(shape, lambda i: (0,) * len(shape))
-    total = sum(piece.size for piece in flat)
+    total = sum(table.size // half for table in tables) * rows
+    sums = pl.BlockSpec((2, block, half), lambda i: (0, i, 0))
+    if last:
+        out_spec = pl.BlockSpec((block, 2 * half), lambda i: (i, 0))
+        out_shape = jax.ShapeDtypeStruct((rows, 2 * half), jnp.bfloat16)
+    else:
+        out_spec = sums
+        out_shape = jax.ShapeDtypeStruct((2, rows, half), jnp.float32)
     return pl.pallas_call(
-        functools.partial(inverse_kernel, dists=dists, chunks=len(hemis)),
+        functools.partial(
+            inverse_kernel,
+            levs=levs,
+            dists=dists,
+            chunks=len(hemis),
+            first=before is None,
+            last=last,
+        ),
         grid=(rows // block,),
-        in_specs=[pl.BlockSpec(piece.shape[:3] + (block,), lambda i: (0, 0, 0, i)) for piece in flat]
-        + [whole(table.shape) for table in tables],
-        out_specs=pl.BlockSpec((block, 2 * half), lambda i: (i, 0)),
-        out_shape=jax.ShapeDtypeStruct((rows, 2 * half), jnp.bfloat16),
+        in_specs=specs
+        + [whole(table.shape) for table in tables]
+        + [sums] * (before is not None),
+        out_specs=out_spec,
+        out_shape=out_shape,
+        compiler_params=pltpu.CompilerParams(vmem_limit_bytes=VMEM_LIMIT),
         cost_estimate=pl.CostEstimate(
             flops=2 * total * half,
-            bytes_accessed=2 * total + 2 * sum(t.size for t in tables) + 4 * rows * half,
+            bytes_accessed=2 * total + 2 * sum(t.size for t in tables) + 8 * rows * half,
             transcendentals=0,
         ),
-    )(*flat, *tables)
+    )(*flat, *tables, *([] if before is None else [before]))
+
+
+def regroup_kernel(*refs):
+    *refs, arrived = refs
+    count = refs[0].shape[0]
+    pieces, outs = refs[: len(refs) - count + 1], refs[len(refs) - count + 1 :]
+    copies = [
+        pltpu.make_async_copy(piece.at[index + 1], out.at[source], arrived.at[index, source])
+        for index, out in enumerate(outs)
+        for source, piece in enumerate(pieces)
+    ]
+    for copy in copies:
+        copy.start()
+    for copy in copies:
+        copy.wait()
+
+
+def regroup(pieces):
+    count, rest = pieces[0].shape[0], pieces[0].shape[1:]
+    size = pieces[0].dtype.itemsize * math.prod(rest) * len(pieces) * (count - 1)
+    return pl.pallas_call(
+        regroup_kernel,
+        in_specs=[pl.BlockSpec(memory_space=pl.ANY)] * len(pieces),
+        out_shape=[jax.ShapeDtypeStruct((len(pieces),) + rest, pieces[0].dtype)] * (count - 1),
+        scratch_shapes=[pltpu.SemaphoreType.DMA((count - 1, len(pieces)))],
+        compiler_params=pltpu.CompilerParams(vmem_limit_bytes=VMEM_LIMIT),
+        cost_estimate=pl.CostEstimate(flops=0, bytes_accessed=2 * size, transcendentals=0),
+    )(*pieces)
 
 
 def in_three(matrix):
@@ -212,7 +285,9 @@
     numbers, *refs, lats, dists, lev_count, wave_count, slots, first_slot, lat_at, together
 ):
     near, far = refs[:dists], refs[dists : dists + lev_count - 1]
-    table, analysis, synthesis, rate, out, work, lines_in = refs[dists + lev_count - 1 :]
+    table, analysis, synthesis, rate, out, work, lines_in, pieces, arrived = refs[
+        dists + lev_count - 1 :
+    ]
     slots_all = lat_at
     slot = pl.program_id(0)
     tall = 2 * slots
@@ -221,10 +296,7 @@
     rows = 2 * group
 
     def piece(dist, parity, lev, line):
-        there = slice(line * lats, (line + 1) * lats)
-        if lev == 0:
-            return near[dist][0, parity, :, there]
-        return far[lev - 1][dist, parity, :, there]
+        return pieces[lev, dist, parity, :, line * lats : (line + 1) * lats]
 
     def place(dist, parity, lev, line):
         at = (((dist * 2 + parity) * lev_count + lev) * lines + line) * tall
@@ -240,6 +312,17 @@
 
     @pl.when(slot == 0)
     def _():
+        copies = [
+            pltpu.make_async_copy(ref.at[0], pieces.at[0, dist], arrived.at[dist])
+            for dist, ref in enumerate(near)
+        ] + [
+            pltpu.make_async_copy(ref, pieces.at[lev + 1], arrived.at[dists + lev])
+            for lev, ref in enumerate(far)
+        ]
+        for copy in copies:
+            copy.start()
+        for copy in copies:
+            copy.wait()
         for at in every:
             work[place(*at), :] = piece(*at).astype(jnp.float32)
 
@@ -248,6 +331,10 @@
     cols = table.shape[3]
     column = lax.broadcasted_iota(jnp.int32, (1, cols), 1)
     lane = lax.broadcasted_iota(jnp.int32, (1, lats), 1)
+    modes = rate.shape[1]
+    across = lax.broadcasted_iota(jnp.int32, (modes, modes), 1)
+    down = lax.broadcasted_iota(jnp.int32, (modes, modes), 0)
+    rates = jnp.sum(jnp.where(across == down, rate[...], 0.0), axis=1, keepdims=True)
 
     def rows_at(slot, block, parity, part):
         dist = block ^ lat_here
@@ -270,14 +357,13 @@
                         keep, value, 0.0
                     ).astype(lines_in.dtype)
 
-    def mix(matrix, value):
+    def parts_of(value):
         high = value.astype(jnp.bfloat16)
         low = (value - high.astype(jnp.float32)).astype(jnp.bfloat16)
-        return jnp.dot(
-            matrix[...],
-            jnp.concatenate([high, low, high], axis=0),
-            preferred_element_type=jnp.float32,
-        )
+        return jnp.concatenate([high, low, high], axis=0)
+
+    def mix(matrix, parts):
+        return jnp.dot(matrix[...], parts, preferred_element_type=jnp.float32)
 
     def transform(slot, lines_in, legendre):
         first = numbers[first_slot + slot]
@@ -285,6 +371,8 @@
         first_odd = (first & 1) == 1
         count_one = ((wave_count - 1 - first - parity_here) >> 1) + 1
         count_two = jnp.maximum(((first - parity_here) >> 1) + 1, 0)
+        both = jnp.dot(lines_in[...], legendre[...], preferred_element_type=jnp.float32)
+        yield
         degree = jnp.where(
             column < count_one,
             first + parity_here + 2 * column,
@@ -296,19 +384,26 @@
         odd_to = jnp.where(first_odd, count_one, count_one + count_two)
         in_even = (column >= even_from) & (column < even_to)
         in_odd = (column >= odd_from) & (column < odd_to)
-        both = jnp.dot(lines_in[...], legendre[...], preferred_element_type=jnp.float32)
-        spectral = jnp.where(in_even, both[:rows], both[rows:])
+        parts = parts_of(jnp.where(in_even, both[:rows], both[rows:]))
+        yield
+        mixed = mix(analysis, parts).reshape(2, rows // 2, cols)
+        yield
         level_deg = degree.astype(jnp.float32)
         growth = level_deg * (level_deg + 1.0) / float(wave_count * wave_count)
-        factor = 1.0 / (1.0 + growth * rate[...])
-        mixed = mix(analysis, spectral).reshape(2, rows // 2, cols)
-        coupled = mix(synthesis, (mixed * factor[None]).reshape(rows, cols))
+        factor = 1.0 / (1.0 + growth * rates)
+        parts = parts_of((mixed * factor[None]).reshape(rows, cols))
+        yield
+        coupled = mix(synthesis, parts)
+        yield
         split = jnp.concatenate(
             [jnp.where(in_even, coupled, 0.0), jnp.where(in_odd, coupled, 0.0)], axis=0
         ).astype(jnp.bfloat16)
-        return lax.dot_general(
+        yield
+        back = lax.dot_general(
             split, legendre[...], (((1,), (1,)), ((), ())), preferred_element_type=jnp.float32
         )
+        yield
+        scatter(slot, back)
 
     def scatter(slot, back):
         starts = starts_of(slot)
@@ -328,9 +423,10 @@
     here = [slot * together + sub for sub in range(together)]
     for sub in range(together):
         gather(here[sub], lines_in.at[sub])
-    backs = [transform(here[sub], lines_in.at[sub], table.at[sub, 0]) for sub in range(together)]
-    for sub in range(together):
-        scatter(here[sub], backs[sub])
+    chains = [transform(here[sub], lines_in.at[sub], table.at[sub, 0]) for sub in range(together)]
+    done = object()
+    while any([next(chain, done) is not done for chain in chains]):
+        pass
 
     @pl.when(slot == slots // together - 1)
     def _():
@@ -366,10 +462,7 @@
         grid_spec=pltpu.PrefetchScalarGridSpec(
             num_scalar_prefetch=1,
             grid=(slots // together,),
-            in_specs=[
-                pl.BlockSpec((1, parities, tall, width), lambda i, n: (0, 0, 0, 0)) for _ in near
-            ]
-            + [whole(piece.shape) for piece in far]
+            in_specs=[pl.BlockSpec(memory_space=pl.ANY)] * (len(near) + len(far))
             + [
                 pl.BlockSpec(
                     (together, 1, lat_total, cols),
@@ -383,9 +476,12 @@
             scratch_shapes=[
                 pltpu.VMEM((dists * rows * tall, lats), jnp.float32),
                 pltpu.VMEM((together, 2 * rows, lat_total), jnp.bfloat16),
+                pltpu.VMEM(shape, jnp.bfloat16),
+                pltpu.SemaphoreType.DMA((len(near) + len(far),)),
             ],
         ),
         out_shape=jax.ShapeDtypeStruct(shape, jnp.bfloat16),
+        compiler_params=pltpu.CompilerParams(vmem_limit_bytes=VMEM_LIMIT),
         cost_estimate=pl.CostEstimate(
             flops=slots * (2 * 2 * 2 * rows * lat_total * cols + 2 * 2 * 3 * rows * rows * cols),
             bytes_accessed=slots * lat_total * cols * 2 + 4 * math.prod(shape),
@@ -422,7 +518,9 @@
     pair_at = pick(pair_order, jnp.concatenate(indices))
     odd_at = jnp.concatenate(odds)
     all_waves = jnp.where((pair_at & 1) == odd_at, pair_at, wave_count - 1 - pair_at)
-    all_waves = jnp.broadcast_to(all_waves[:, None], (all_waves.shape[0], LANES))
+    all_waves = jnp.broadcast_to(all_waves[:, None], (all_waves.shape[0], LANES)).reshape(
+        len(sizes), lat_count, 2, -1, LANES
+    )
 
     own_first = lax.dynamic_slice_in_dim(
         pair_order, (lat_here * lev_count + lev_here) * slots_here, slots_here
@@ -448,30 +546,29 @@
     part_eye = jnp.eye(2, dtype=jnp.float32)
     analysis = in_three(jnp.kron(part_eye, exact(mode_analysis, select)))
     synthesis = in_three(jnp.kron(part_eye, exact(select.T, mode_synthesis)))
-    rate = mode_rate[:, None]
-
-    even, odd = folded_products(grid_state)
+    rate = mode_rate[None, :]
+
     sign_own = (1 - 2 * parity).astype(jnp.float32)
+    mirror = swap_with(grid_state, "fld", 1, False)
+    mirror, numbers, analysis, synthesis, all_waves = lax.optimization_barrier(
+        (mirror, numbers, analysis, synthesis, all_waves)
+    )
+    grid_state = pltpu.with_memory_space_constraint(grid_state, pltpu.HBM)
+    even, odd = folded_products(grid_state, mirror, 1 - 2 * parity)
 
     def combine(partner, own):
         return (partner.astype(jnp.float32) + sign_own * own.astype(jnp.float32)).astype(
             jnp.bfloat16
         )
 
+    legendre = pltpu.with_memory_space_constraint(legendre, pltpu.HBM)
     tables, incoming = [], []
     for chunk, slots in enumerate(sizes):
-        size = lat_count * 2 * lev_count * slots
-        at = lat_count * 2 * lev_count * firsts[chunk]
-        waves = all_waves[at : at + size].reshape(lat_count, 2, -1, LANES)
-        fourier, table = forward_stage(waves, even, odd, slots, lon_count)
-        tables.append(table)
-        mirror = swap_with(fourier, "fld", 1)
-        near = [combine(mirror[dist], fourier[dist]) for dist in range(lat_count)]
+        *near, table = forward_stage(all_waves, chunk, even, odd, slots, lon_count)
+        tables.append(pltpu.with_memory_space_constraint(table, pltpu.HBM))
         near = [swap_with(piece, "lat", dist) for dist, piece in enumerate(near)]
-        far = [
-            swap_with(jnp.stack([block[dist] for block in near]), "lev", dist)
-            for dist in range(1, lev_count)
-        ]
+        far = regroup(near)
+        far = [swap_with(piece, "lev", dist + 1) for dist, piece in enumerate(far)]
         incoming.append((near, far))
     hemis = []
     for chunk, slots in enumerate(sizes):
@@ -487,18 +584,16 @@
             slots,
             firsts[chunk],
         )
-        partner = swap_with(returned, "fld", 1)
-        arrived = [
-            swap_with(combine(partner[dist], returned[dist]), "lev", dist)
-            for dist in range(lev_count)
-        ]
-        hemis.append(
-            [
-                swap_with(jnp.stack([block[dist] for block in arrived]), "lat", dist)
-                for dist in range(lat_count)
-            ]
-        )
-    grid_out = inverse_stage(hemis, tables)
+        partner = swap_with(returned, "fld", 1, False)
+        arrived = [combine(partner[dist], returned[dist]) for dist in range(lev_count)]
+        arrived = [swap_with(piece, "lev", dist) for dist, piece in enumerate(arrived)]
+        far = regroup(arrived)
+        far = [swap_with(piece, "lat", dist + 1) for dist, piece in enumerate(far)]
+        hemis.append((arrived, far))
+    sums = None
+    if len(hemis) > 1:
+        sums = inverse_stage(hemis[:-1], tables[:-1], None, False)
+    grid_out = inverse_stage(hemis[-1:], tables[-1:], sums, True)
     return grid_out.reshape(field_count, levels_here, 1, lats_here, lon_count)
 
 

time: 341 us -> 282 us (0.83)
  other arithmetic: 27.3 us -> 10.3 us
  waiting for transfers between devices: 101 us -> 85.1 us
  local copies, waits for them, and re-layouts: 13.9 us -> 1.03 us
  starting transfers between devices: 119 us -> 108 us
    ppermute x56 -> x53, waiting for transfers between devices: 101 us -> 85.1 us  [swap_with(): value = lax.ppermute(value, axis, pairs)]
    another operation x28 -> x0, other arithmetic: 14.6 us -> none  [the longest x12 11.2 us: local(): jnp.stack([block[dist] for block in near])]
    pallas_call x2 -> x11, Pallas kernels: 14.3 us -> 27.2 us  [the longest x2 12.3 us: inverse_stage(): pl.pallas_call(functools.partial(inverse_kernel, levs=levs, dists=dists,...]
    ppermute x56 -> x53, starting transfers between devices: 119 us -> 108 us  [swap_with(): value = lax.ppermute(value, axis, pairs)]
    pallas_call x4, Pallas kernels: 42.4 us -> 33.6 us  [legendre_stage(): pl.pallas_call(functools.partial(legendre_kernel, lats=lats, dists=dists,...]
    slice x33 -> x0, local copies, waits for them, and re-layouts: 5.95 us -> none  [the longest x32 5.93 us: local(): block[dist]]
    pallas_call x4, Pallas kernels: 18.3 us -> 12.9 us  [forward_stage(): pl.pallas_call(functools.partial(forward_kernel, slots=slots, lon_count=l...]
    convert_element_type x8 -> x4, other arithmetic: 8.07 us -> 6.76 us  [combine(): (partner.astype(jnp.float32) + sign_own * own.astype(jnp.float32)).astype...]
  transfers between devices with their start and end apart: 56 -> 53, of which waited for: 19 -> 19; matrix products, arithmetic and copies ran while one was open for 11% -> 4% of each run, Pallas kernels for 17% -> 21%
where the time goes in v1:
time: 282 us; the launch traced here: 280 us
  starting transfers between devices  108 us (38%)
  waiting for transfers between devices  85.1 us (30%)
  Pallas kernels  73.7 us (26%)
  other arithmetic  10.3 us (4%)
    ppermute x53, starting transfers between devices, swap_with(): value = lax.ppermute(value, axis, pairs)  108 us
    ppermute x53, waiting for transfers between devices, swap_with(): value = lax.ppermute(value, axis, pairs)  85.1 us
    pallas_call x4, Pallas kernels, legendre_stage(): pl.pallas_call(functools.partial(legendre_kernel, lats=lats, dists=dists,...  33.6 us
    pallas_call x4, Pallas kernels, forward_stage(): pl.pallas_call(functools.partial(forward_kernel, slots=slots, lon_count=l...  12.9 us
    pallas_call x2, Pallas kernels, inverse_stage(): pl.pallas_call(functools.partial(inverse_kernel, levs=levs, dists=dists,...  12.3 us
    pallas_call x8, Pallas kernels, regroup(): pl.pallas_call(regroup_kernel, in_specs=[pl.BlockSpec(memory_space=pl.ANY...  8.96 us
    convert_element_type x4, other arithmetic, combine(): (partner.astype(jnp.float32) + sign_own * own.astype(jnp.float32)).astype...  6.76 us
    pallas_call x1, Pallas kernels, folded_products(): pl.pallas_call(fold_kernel, grid_spec=pltpu.PrefetchScalarGridSpec(num_sc...  5.99 us
  transfers between devices with their start and end apart: 53, of which 19 were waited for; matrix products, arithmetic and copies ran while one was open for 4% of the time, Pallas kernels for 21%

profile of v1, /device:TPU:0, one launch (start us, length us, event | category | flops | bytes accessed | tf_op | source)
XLA Modules:
  0.0 279.6 jit_solution(16718590444638319703)
XLA Ops:
  7.8 6.0 %shard_map.73 = (bf16[2,512,1024]{2,1,0:T(8,128)(2,1)S(1)}, bf16[2,512,1024]{2,1,0:T(8,128)(2,1)S(1)}) custom-call(s32[1]{0:T(128)} %bitcast.3.sign, bf16[2,4,1,128,2048]{4,3,2,1,0:T(8,128)(2,1)} %own.1, bf16[2,4,1,128,2048]{4,3,2,1,0:T(8,128)(2,1)} %collective-permute-done.mirror), custom_call_target="tpu_custom_call" | custom-call | flops 16777216 | bytes 12582912 | tf_op jit(solution)/shard_map/pallas_call | solution.py:67
  13.8 3.2 %shard_map.86 = (bf16[4,2,16,1024]{3,2,1,0:T(8,128)(2,1)S(1)}, bf16[4,2,16,1024]{3,2,1,0:T(8,128)(2,1)S(1)}, bf16[4,2,16,1024]{3,2,1,0:T(8,128)(2,1)S(1)}, bf16[...) custom-call(s32[4,4,2,32,128]{4,3,2,1,0:T(8,128)S(1)} %broadcast_in_dim.56.waves, bf16[1024,1024]{1,0:T(8,128)(2,1)S(1)} %bitcast.45, ...), custom_call_target="tpu_custom_call" | custom-call | flops 1073741824 | bytes 6291456 | tf_op jit(solution)/shard_map/pallas_call | solution.py:158
  17.0 2.9 %collective-permute-start.40 = (bf16[4,2,16,1024]{3,2,1,0:T(8,128)(2,1)S(1)}, bf16[4,2,16,1024]{3,2,1,0:T(8,128)(2,1)S(1)}, u32[]{:S(2)}, u32[]{:S(2)}) collective-permute-start(bf16[4,2,16,1024]{3,2,1,0:T(8,128)(2,1)S(1)} %get-tuple-element.95), channel_id=1, source_target_pairs={{0,8},{8,0},{16,24},{24,16},{1,9},{9,1},{17,25},{25,17},{2,10},{10... | collective-permute-start | bytes 786440 | tf_op jit(solution)/shard_map/ppermute | solution.py:20
  22.6 3.2 %shard_map.82 = (bf16[4,2,16,1024]{3,2,1,0:T(8,128)(2,1)S(1)}, bf16[4,2,16,1024]{3,2,1,0:T(8,128)(2,1)S(1)}, bf16[4,2,16,1024]{3,2,1,0:T(8,128)(2,1)S(1)}, bf16[...) custom-call(s32[4,4,2,32,128]{4,3,2,1,0:T(8,128)S(1)} %broadcast_in_dim.56.waves, bf16[1024,1024]{1,0:T(8,128)(2,1)S(1)} %bitcast.46, ...), custom_call_target="tpu_custom_call" | custom-call | flops 1073741824 | bytes 6291456 | tf_op jit(solution)/shard_map/pallas_call | solution.py:158
  26.7 3.5 %collective-permute-start.28 = (bf16[4,2,16,1024]{3,2,1,0:T(8,128)(2,1)S(1)}, bf16[4,2,16,1024]{3,2,1,0:T(8,128)(2,1)S(1)}, u32[]{:S(2)}, u32[]{:S(2)}) collective-permute-start(bf16[4,2,16,1024]{3,2,1,0:T(8,128)(2,1)S(1)} %get-tuple-element.86), channel_id=1, source_target_pairs={{0,16},{8,24},{16,0},{24,8},{1,17},{9,25},{17,1},{25,9},{2,18},{10... | collective-permute-start | bytes 786440 | tf_op jit(solution)/shard_map/ppermute | solution.py:20
  30.2 3.2 %shard_map.78 = (bf16[4,2,16,1024]{3,2,1,0:T(8,128)(2,1)S(1)}, bf16[4,2,16,1024]{3,2,1,0:T(8,128)(2,1)S(1)}, bf16[4,2,16,1024]{3,2,1,0:T(8,128)(2,1)S(1)}, bf16[...) custom-call(s32[4,4,2,32,128]{4,3,2,1,0:T(8,128)S(1)} %broadcast_in_dim.56.waves, bf16[1024,1024]{1,0:T(8,128)(2,1)S(1)} %bitcast.47, ...), custom_call_target="tpu_custom_call" | custom-call | flops 1073741824 | bytes 6291456 | tf_op jit(solution)/shard_map/pallas_call | solution.py:158
  33.4 2.7 collective-permute-start.29
  36.1 5.2 %collective-permute-done.41.refs_2_ = bf16[4,2,16,1024]{3,2,1,0:T(8,128)(2,1)S(1)} collective-permute-done((bf16[4,2,16,1024]{3,2,1,0:T(8,128)(2,1)S(1)}, bf16[4,2,16,1024]{3,2,1,0:T(8,128)(2,1)S(1)}, u32[]{:S(2)}, u32[]{:S(2)}) %collective-permute-start.41) | collective-permute-done | bytes 262176 | tf_op jit(solution)/shard_map/ppermute | solution.py:20
  41.3 18.4 %collective-permute-start.15 = (bf16[4,2,16,1024]{3,2,1,0:T(8,128)(2,1)S(1)}, bf16[4,2,16,1024]{3,2,1,0:T(8,128)(2,1)S(1)}, u32[]{:S(2)}, u32[]{:S(2)}) collective-permute-start(bf16[4,2,16,1024]{3,2,1,0:T(8,128)(2,1)S(1)} %get-tuple-element.76), channel_id=1, source_target_pairs={{0,16},{8,24},{16,0},{24,8},{1,17},{9,25},{17,1},{25,9},{2,18},{10... | collective-permute-start | bytes 786440 | tf_op jit(solution)/shard_map/ppermute | solution.py:20
  62.2 12.8 %collective-permute-done.28.refs_2_ = bf16[4,2,16,1024]{3,2,1,0:T(8,128)(2,1)S(1)} collective-permute-done((bf16[4,2,16,1024]{3,2,1,0:T(8,128)(2,1)S(1)}, bf16[4,2,16,1024]{3,2,1,0:T(8,128)(2,1)S(1)}, u32[]{:S(2)}, u32[]{:S(2)}) %collective-permute-start.28) | collective-permute-done | bytes 262176 | tf_op jit(solution)/shard_map/ppermute | solution.py:20
  78.5 3.3 %shard_map.74 = (bf16[4,2,16,1024]{3,2,1,0:T(8,128)(2,1)S(1)}, bf16[4,2,16,1024]{3,2,1,0:T(8,128)(2,1)S(1)}, bf16[4,2,16,1024]{3,2,1,0:T(8,128)(2,1)S(1)}, bf16[...) custom-call(s32[4,4,2,32,128]{4,3,2,1,0:T(8,128)S(1)} %broadcast_in_dim.56.waves, bf16[1024,1024]{1,0:T(8,128)(2,1)S(1)} %bitcast.48, ...), custom_call_target="tpu_custom_call" | custom-call | flops 1073741824 | bytes 6291456 | tf_op jit(solution)/shard_map/pallas_call | solution.py:158
  81.8 4.5 %collective-permute-done.15.refs_2_ = bf16[4,2,16,1024]{3,2,1,0:T(8,128)(2,1)S(1)} collective-permute-done((bf16[4,2,16,1024]{3,2,1,0:T(8,128)(2,1)S(1)}, bf16[4,2,16,1024]{3,2,1,0:T(8,128)(2,1)S(1)}, u32[]{:S(2)}, u32[]{:S(2)}) %collective-permute-start.15) | collective-permute-done | bytes 262176 | tf_op jit(solution)/shard_map/ppermute | solution.py:20
  87.4 5.0 %collective-permute-start.2 = (bf16[4,2,16,1024]{3,2,1,0:T(8,128)(2,1)S(1)}, bf16[4,2,16,1024]{3,2,1,0:T(8,128)(2,1)S(1)}, u32[]{:S(2)}, u32[]{:S(2)}) collective-permute-start(bf16[4,2,16,1024]{3,2,1,0:T(8,128)(2,1)S(1)} %get-tuple-element.63), channel_id=1, source_target_pairs={{0,16},{8,24},{16,0},{24,8},{1,17},{9,25},{17,1},{25,9},{2,18},{10... | collective-permute-start | bytes 786440 | tf_op jit(solution)/shard_map/ppermute | solution.py:20
  97.1 8.1 %shard_map.88 = bf16[4,4,2,16,1024]{4,3,2,1,0:T(8,128)(2,1)S(1)} custom-call(s32[98]{0:T(128)S(1)} %pad_add_fusion.2.numbers, bf16[4,2,16,1024]{3,2,1,0:T(8,128)(2,1)S(1)} %get-tuple-element.94.refs_0_, bf16[4,2,16,1024]{3,2,1,0:T(8,128)(2,1)S(1)} %collective-permute-done.40.refs_1_, bf16[4,2,16,1024]{3,2,1,0:T(8,128)(2,1)S(1)} %collective-permute-done.41.refs_2_, ...), custom_call_target="tpu_custom_call" | custom-call | flops 1593835520 | bytes 7340032 | tf_op jit(solution)/shard_map/pallas_call | solution.py:450
  111.4 8.1 %shard_map.84 = bf16[4,4,2,16,1024]{4,3,2,1,0:T(8,128)(2,1)S(1)} custom-call(s32[98]{0:T(128)S(1)} %pad_add_fusion.2.numbers, bf16[4,2,16,1024]{3,2,1,0:T(8,128)(2,1)S(1)} %get-tuple-element.84.refs_0_, bf16[4,2,16,1024]{3,2,1,0:T(8,128)(2,1)S(1)} %collective-permute-done.27.refs_1_, bf16[4,2,16,1024]{3,2,1,0:T(8,128)(2,1)S(1)} %collective-permute-done.28.refs_2_, ...), custom_call_target="tpu_custom_call" | custom-call | flops 1593835520 | bytes 7340032 | tf_op jit(solution)/shard_map/pallas_call | solution.py:450
  124.6 8.3 %shard_map.80 = bf16[4,4,2,16,1024]{4,3,2,1,0:T(8,128)(2,1)S(1)} custom-call(s32[98]{0:T(128)S(1)} %pad_add_fusion.2.numbers, bf16[4,2,16,1024]{3,2,1,0:T(8,128)(2,1)S(1)} %get-tuple-element.74.refs_0_, bf16[4,2,16,1024]{3,2,1,0:T(8,128)(2,1)S(1)} %collective-permute-done.14.refs_1_, bf16[4,2,16,1024]{3,2,1,0:T(8,128)(2,1)S(1)} %collective-permute-done.15.refs_2_, ...), custom_call_target="tpu_custom_call" | custom-call | flops 1593835520 | bytes 7340032 | tf_op jit(solution)/shard_map/pallas_call | solution.py:450
  133.0 3.3 %collective-permute-done.5.refs_5_ = bf16[4,2,16,1024]{3,2,1,0:T(8,128)(2,1)S(1)} collective-permute-done((bf16[4,2,16,1024]{3,2,1,0:T(8,128)(2,1)S(1)}, bf16[4,2,16,1024]{3,2,1,0:T(8,128)(2,1)S(1)}, u32[]{:S(2)}, u32[]{:S(2)}) %collective-permute-start.5) | collective-permute-done | bytes 262176 | tf_op jit(solution)/shard_map/ppermute | solution.py:20
  136.4 9.1 %shard_map.76 = bf16[4,4,2,16,1024]{4,3,2,1,0:T(8,128)(2,1)} custom-call(s32[98]{0:T(128)S(1)} %pad_add_fusion.2.numbers, bf16[4,2,16,1024]{3,2,1,0:T(8,128)(2,1)S(1)} %get-tuple-element.61.refs_0_, bf16[4,2,16,1024]{3,2,1,0:T(8,128)(2,1)S(1)} %collective-permute-done.1.refs_1_, bf16[4,2,16,1024]{3,2,1,0:T(8,128)(2,1)S(1)} %collective-permute-done.2.refs_2_, ...), custom_call_target="tpu_custom_call" | custom-call | flops 1593835520 | bytes 7340032 | tf_op jit(solution)/shard_map/pallas_call | solution.py:450
  165.7 2.9 %collective-permute-done.36.refs_3_.refs_10_ = bf16[4,2,16,1024]{3,2,1,0:T(8,128)(2,1)S(1)} collective-permute-done((bf16[4,2,16,1024]{3,2,1,0:T(8,128)(2,1)S(1)}, bf16[4,2,16,1024]{3,2,1,0:T(8,128)(2,1)S(1)}, u32[]{:S(2)}, u32[]{:S(2)}) %collective-permute-start.36) | collective-permute-done | bytes 262176 | tf_op jit(solution)/shard_map/ppermute | solution.py:20
  169.9 4.3 %collective-permute-done.35.refs_2_.refs_9_ = bf16[4,2,16,1024]{3,2,1,0:T(8,128)(2,1)S(1)} collective-permute-done((bf16[4,2,16,1024]{3,2,1,0:T(8,128)(2,1)S(1)}, bf16[4,2,16,1024]{3,2,1,0:T(8,128)(2,1)S(1)}, u32[]{:S(2)}, u32[]{:S(2)}) %collective-permute-start.35) | collective-permute-done | bytes 262176 | tf_op jit(solution)/shard_map/ppermute | solution.py:20
  181.1 4.3 %collective-permute-done.22.refs_2_ = bf16[4,2,16,1024]{3,2,1,0:T(8,128)(2,1)S(1)} collective-permute-done((bf16[4,2,16,1024]{3,2,1,0:T(8,128)(2,1)S(1)}, bf16[4,2,16,1024]{3,2,1,0:T(8,128)(2,1)S(1)}, u32[]{:S(2)}, u32[]{:S(2)}) %collective-permute-start.22) | collective-permute-done | bytes 262176 | tf_op jit(solution)/shard_map/ppermute | solution.py:20
  185.6 2.9 %collective-permute-start.51 = (bf16[4,2,16,1024]{3,2,1,0:T(8,128)(2,1)S(1)}, bf16[4,2,16,1024]{3,2,1,0:T(8,128)(2,1)S(1)}, u32[]{:S(2)}, u32[]{:S(2)}) collective-permute-start(bf16[4,2,16,1024]{3,2,1,0:T(8,128)(2,1)S(1)} %get-tuple-element.102), channel_id=1, source_target_pairs={{0,16},{8,24},{16,0},{24,8},{1,17},{9,25},{17,1},{25,9},{2,18},{10... | collective-permute-start | bytes 786440 | tf_op jit(solution)/shard_map/ppermute | solution.py:20
  188.4 2.7 collective-permute-done.10.refs_3_
  197.3 3.1 %collective-permute-start.38 = (bf16[4,2,16,1024]{3,2,1,0:T(8,128)(2,1)S(1)}, bf16[4,2,16,1024]{3,2,1,0:T(8,128)(2,1)S(1)}, u32[]{:S(2)}, u32[]{:S(2)}) collective-permute-start(bf16[4,2,16,1024]{3,2,1,0:T(8,128)(2,1)S(1)} %get-tuple-element.92), channel_id=1, source_target_pairs={{0,16},{8,24},{16,0},{24,8},{1,17},{9,25},{17,1},{25,9},{2,18},{10... | collective-permute-start | bytes 786440 | tf_op jit(solution)/shard_map/ppermute | solution.py:20
  201.7 5.2 %collective-permute-done.51.refs_19_ = bf16[4,2,16,1024]{3,2,1,0:T(8,128)(2,1)S(1)} collective-permute-done((bf16[4,2,16,1024]{3,2,1,0:T(8,128)(2,1)S(1)}, bf16[4,2,16,1024]{3,2,1,0:T(8,128)(2,1)S(1)}, u32[]{:S(2)}, u32[]{:S(2)}) %collective-permute-start.51) | collective-permute-done | bytes 262176 | tf_op jit(solution)/shard_map/ppermute | solution.py:20
  207.0 18.5 %collective-permute-start.25 = (bf16[4,2,16,1024]{3,2,1,0:T(8,128)(2,1)S(1)}, bf16[4,2,16,1024]{3,2,1,0:T(8,128)(2,1)S(1)}, u32[]{:S(2)}, u32[]{:S(2)}) collective-permute-start(bf16[4,2,16,1024]{3,2,1,0:T(8,128)(2,1)S(1)} %get-tuple-element.82), channel_id=1, source_target_pairs={{0,16},{8,24},{16,0},{24,8},{1,17},{9,25},{17,1},{25,9},{2,18},{10... | collective-permute-start | bytes 786440 | tf_op jit(solution)/shard_map/ppermute | solution.py:20
  227.8 12.8 %collective-permute-done.38.refs_12_ = bf16[4,2,16,1024]{3,2,1,0:T(8,128)(2,1)S(1)} collective-permute-done((bf16[4,2,16,1024]{3,2,1,0:T(8,128)(2,1)S(1)}, bf16[4,2,16,1024]{3,2,1,0:T(8,128)(2,1)S(1)}, u32[]{:S(2)}, u32[]{:S(2)}) %collective-permute-start.38) | collective-permute-done | bytes 262176 | tf_op jit(solution)/shard_map/ppermute | solution.py:20
  240.7 7.3 %collective-permute-start.12 = (bf16[4,2,16,1024]{3,2,1,0:T(8,128)(2,1)S(1)}, bf16[4,2,16,1024]{3,2,1,0:T(8,128)(2,1)S(1)}, u32[]{:S(2)}, u32[]{:S(2)}) collective-permute-start(bf16[4,2,16,1024]{3,2,1,0:T(8,128)(2,1)S(1)} %get-tuple-element.71), channel_id=1, source_target_pairs={{0,16},{8,24},{16,0},{24,8},{1,17},{9,25},{17,1},{25,9},{2,18},{10... | collective-permute-start | bytes 786440 | tf_op jit(solution)/shard_map/ppermute | solution.py:20
  249.2 14.0 %collective-permute-done.25.refs_5_ = bf16[4,2,16,1024]{3,2,1,0:T(8,128)(2,1)S(1)} collective-permute-done((bf16[4,2,16,1024]{3,2,1,0:T(8,128)(2,1)S(1)}, bf16[4,2,16,1024]{3,2,1,0:T(8,128)(2,1)S(1)}, u32[]{:S(2)}, u32[]{:S(2)}) %collective-permute-start.25) | collective-permute-done | bytes 262176 | tf_op jit(solution)/shard_map/ppermute | solution.py:20
  263.2 7.1 %shard_map.90.refs_8_ = f32[2,1024,1024]{2,1,0:T(8,128)S(1)} custom-call(bf16[4,2,16,1024]{3,2,1,0:T(8,128)(2,1)S(1)} %get-tuple-element.125.refs_0_, bf16[4,2,16,1024]{3,2,1,0:T(8,128)(2,1)S(1)} %collective-permute-done.21.refs_1_, bf16[4,2,16,1024]{3,2,1,0:T(8,128)(2,1)S(1)} %collective-permute-done.22.refs_2_, ...), custom_call_target="tpu_custom_call" | custom-call | flops 3221225472 | bytes 14680064 | tf_op jit(solution)/shard_map/pallas_call | solution.py:226
  270.3 4.1 %collective-permute-done.12.refs_5_ = bf16[4,2,16,1024]{3,2,1,0:T(8,128)(2,1)S(1)} collective-permute-done((bf16[4,2,16,1024]{3,2,1,0:T(8,128)(2,1)S(1)}, bf16[4,2,16,1024]{3,2,1,0:T(8,128)(2,1)S(1)}, u32[]{:S(2)}, u32[]{:S(2)}) %collective-permute-start.12) | collective-permute-done | bytes 262176 | tf_op jit(solution)/shard_map/ppermute | solution.py:20
  274.4 5.2 %shard_map.91 = bf16[1024,2048]{1,0:T(8,128)(2,1)} custom-call(bf16[4,2,16,1024]{3,2,1,0:T(8,128)(2,1)S(1)} %get-tuple-element.129.refs_0_, bf16[4,2,16,1024]{3,2,1,0:T(8,128)(2,1)S(1)} %collective-permute-done.8.refs_1_, bf16[4,2,16,1024]{3,2,1,0:T(8,128)(2,1)S(1)} %collective-permute-done.9.refs_2_, ...), custom_call_target="tpu_custom_call" | custom-call | flops 1073741824 | bytes 10485760 | tf_op jit(solution)/shard_map/pallas_call | solution.py:226
  (138 shorter events, 74.0 us)
Async XLA Ops:
  20.0 21.4 %collective-permute-start.41 = (bf16[4,2,16,1024]{3,2,1,0:T(8,128)(2,1)S(1)}, bf16[4,2,16,1024]{3,2,1,0:T(8,128)(2,1)S(1)}, u32[]{:S(2)}, u32[]{:S(2)}) collective-permute-start(bf16[4,2,16,1024]{3,2,1,0:T(8,128)(2,1)S(1)} %get-tuple-element.96), channel_id=1, source_target_pairs={{0,16},{8,24},{16,0},{24,8},{1,17},{9,25},{17,1},{25,9},{2,18},{10... | collective-permute-start | bytes 786440 | tf_op jit(solution)/shard_map/ppermute | solution.py:20
  22.6 18.8 %collective-permute-start.42 = (bf16[4,2,16,1024]{3,2,1,0:T(8,128)(2,1)S(1)}, bf16[4,2,16,1024]{3,2,1,0:T(8,128)(2,1)S(1)}, u32[]{:S(2)}, u32[]{:S(2)}) collective-permute-start(bf16[4,2,16,1024]{3,2,1,0:T(8,128)(2,1)S(1)} %get-tuple-element.97), channel_id=1, source_target_pairs={{0,24},{8,16},{16,8},{24,0},{1,25},{9,17},{17,9},{25,1},{2,26},{10... | collective-permute-start | bytes 786440 | tf_op jit(solution)/shard_map/ppermute | solution.py:20
  25.8 34.0 %collective-permute-start.27 = (bf16[4,2,16,1024]{3,2,1,0:T(8,128)(2,1)S(1)}, bf16[4,2,16,1024]{3,2,1,0:T(8,128)(2,1)S(1)}, u32[]{:S(2)}, u32[]{:S(2)}) collective-permute-start(bf16[4,2,16,1024]{3,2,1,0:T(8,128)(2,1)S(1)} %get-tuple-element.85), channel_id=1, source_target_pairs={{0,8},{8,0},{16,24},{24,16},{1,9},{9,1},{17,25},{25,17},{2,10},{10... | collective-permute-start | bytes 786440 | tf_op jit(solution)/shard_map/ppermute | solution.py:20
  26.7 48.4 %collective-permute-start.28 = (bf16[4,2,16,1024]{3,2,1,0:T(8,128)(2,1)S(1)}, bf16[4,2,16,1024]{3,2,1,0:T(8,128)(2,1)S(1)}, u32[]{:S(2)}, u32[]{:S(2)}) collective-permute-start(bf16[4,2,16,1024]{3,2,1,0:T(8,128)(2,1)S(1)} %get-tuple-element.86), channel_id=1, source_target_pairs={{0,16},{8,24},{16,0},{24,8},{1,17},{9,25},{17,1},{25,9},{2,18},{10... | collective-permute-start | bytes 786440 | tf_op jit(solution)/shard_map/ppermute | solution.py:20
  33.4 43.1 %collective-permute-start.29 = (bf16[4,2,16,1024]{3,2,1,0:T(8,128)(2,1)S(1)}, bf16[4,2,16,1024]{3,2,1,0:T(8,128)(2,1)S(1)}, u32[]{:S(2)}, u32[]{:S(2)}) collective-permute-start(bf16[4,2,16,1024]{3,2,1,0:T(8,128)(2,1)S(1)} %get-tuple-element.87), channel_id=1, source_target_pairs={{0,24},{8,16},{16,8},{24,0},{1,25},{9,17},{17,9},{25,1},{2,26},{10... | collective-permute-start | bytes 786440 | tf_op jit(solution)/shard_map/ppermute | solution.py:20
  41.3 36.7 %collective-permute-start.14 = (bf16[4,2,16,1024]{3,2,1,0:T(8,128)(2,1)S(1)}, bf16[4,2,16,1024]{3,2,1,0:T(8,128)(2,1)S(1)}, u32[]{:S(2)}, u32[]{:S(2)}) collective-permute-start(bf16[4,2,16,1024]{3,2,1,0:T(8,128)(2,1)S(1)} %get-tuple-element.75), channel_id=1, source_target_pairs={{0,8},{8,0},{16,24},{24,16},{1,9},{9,1},{17,25},{25,17},{2,10},{10... | collective-permute-start | bytes 786440 | tf_op jit(solution)/shard_map/ppermute | solution.py:20
  41.3 44.9 %collective-permute-start.15 = (bf16[4,2,16,1024]{3,2,1,0:T(8,128)(2,1)S(1)}, bf16[4,2,16,1024]{3,2,1,0:T(8,128)(2,1)S(1)}, u32[]{:S(2)}, u32[]{:S(2)}) collective-permute-start(bf16[4,2,16,1024]{3,2,1,0:T(8,128)(2,1)S(1)} %get-tuple-element.76), channel_id=1, source_target_pairs={{0,16},{8,24},{16,0},{24,8},{1,17},{9,25},{17,1},{25,9},{2,18},{10... | collective-permute-start | bytes 786440 | tf_op jit(solution)/shard_map/ppermute | solution.py:20
  59.8 27.7 %collective-permute-start.16 = (bf16[4,2,16,1024]{3,2,1,0:T(8,128)(2,1)S(1)}, bf16[4,2,16,1024]{3,2,1,0:T(8,128)(2,1)S(1)}, u32[]{:S(2)}, u32[]{:S(2)}) collective-permute-start(bf16[4,2,16,1024]{3,2,1,0:T(8,128)(2,1)S(1)} %get-tuple-element.77), channel_id=1, source_target_pairs={{0,24},{8,16},{16,8},{24,0},{1,25},{9,17},{17,9},{25,1},{2,26},{10... | collective-permute-start | bytes 786440 | tf_op jit(solution)/shard_map/ppermute | solution.py:20
  75.0 18.5 %collective-permute-start.43 = (bf16[4,2,16,1024]{3,2,1,0:T(8,128)(2,1)S(1)}, bf16[4,2,16,1024]{3,2,1,0:T(8,128)(2,1)S(1)}, u32[]{:S(2)}, u32[]{:S(2)}) collective-permute-start(bf16[4,2,16,1024]{3,2,1,0:T(8,128)(2,1)S(1)} %get-tuple-element.98), channel_id=1, source_target_pairs={{0,2},{2,0},{4,6},{6,4},{1,3},{3,1},{5,7},{7,5},{8,10},{10,8},{12,... | collective-permute-start | bytes 786440 | tf_op jit(solution)/shard_map/ppermute | solution.py:20
  76.5 18.6 %collective-permute-start.44 = (bf16[4,2,16,1024]{3,2,1,0:T(8,128)(2,1)S(1)}, bf16[4,2,16,1024]{3,2,1,0:T(8,128)(2,1)S(1)}, u32[]{:S(2)}, u32[]{:S(2)}) collective-permute-start(bf16[4,2,16,1024]{3,2,1,0:T(8,128)(2,1)S(1)} %get-tuple-element.99), channel_id=1, source_target_pairs={{0,4},{2,6},{4,0},{6,2},{1,5},{3,7},{5,1},{7,3},{8,12},{10,14},{12... | collective-permute-start | bytes 786440 | tf_op jit(solution)/shard_map/ppermute | solution.py:20
  78.1 18.6 %collective-permute-start.45 = (bf16[4,2,16,1024]{3,2,1,0:T(8,128)(2,1)S(1)}, bf16[4,2,16,1024]{3,2,1,0:T(8,128)(2,1)S(1)}, u32[]{:S(2)}, u32[]{:S(2)}) collective-permute-start(bf16[4,2,16,1024]{3,2,1,0:T(8,128)(2,1)S(1)} %get-tuple-element.100), channel_id=1, source_target_pairs={{0,6},{2,4},{4,2},{6,0},{1,7},{3,5},{5,3},{7,1},{8,14},{10,12},{12... | collective-permute-start | bytes 786440 | tf_op jit(solution)/shard_map/ppermute | solution.py:20
  86.3 18.9 %collective-permute-start.1 = (bf16[4,2,16,1024]{3,2,1,0:T(8,128)(2,1)S(1)}, bf16[4,2,16,1024]{3,2,1,0:T(8,128)(2,1)S(1)}, u32[]{:S(2)}, u32[]{:S(2)}) collective-permute-start(bf16[4,2,16,1024]{3,2,1,0:T(8,128)(2,1)S(1)} %get-tuple-element.62), channel_id=1, source_target_pairs={{0,8},{8,0},{16,24},{24,16},{1,9},{9,1},{17,25},{25,17},{2,10},{10... | collective-permute-start | bytes 786440 | tf_op jit(solution)/shard_map/ppermute | solution.py:20
  87.4 17.9 %collective-permute-start.2 = (bf16[4,2,16,1024]{3,2,1,0:T(8,128)(2,1)S(1)}, bf16[4,2,16,1024]{3,2,1,0:T(8,128)(2,1)S(1)}, u32[]{:S(2)}, u32[]{:S(2)}) collective-permute-start(bf16[4,2,16,1024]{3,2,1,0:T(8,128)(2,1)S(1)} %get-tuple-element.63), channel_id=1, source_target_pairs={{0,16},{8,24},{16,0},{24,8},{1,17},{9,25},{17,1},{25,9},{2,18},{10... | collective-permute-start | bytes 786440 | tf_op jit(solution)/shard_map/ppermute | solution.py:20
  105.2 40.3 %collective-permute-start.46 = (bf16[4,4,2,16,1024]{4,3,2,1,0:T(8,128)(2,1)S(1)}, bf16[4,4,2,16,1024]{4,3,2,1,0:T(8,128)(2,1)}, u32[]{:S(2)}, u32[]{:S(2)}) collective-permute-start(bf16[4,4,2,16,1024]{4,3,2,1,0:T(8,128)(2,1)S(1)} %shard_map.88), channel_id=1, source_target_pairs={{0,1},{1,0},{2,3},{3,2},{4,5},{5,4},{6,7},{7,6},{8,9},{9,8},{10,11... | collective-permute-start | bytes 3145736 | tf_op jit(solution)/shard_map/ppermute | solution.py:20
  119.6 30.4 %collective-permute-start.33 = (bf16[4,4,2,16,1024]{4,3,2,1,0:T(8,128)(2,1)S(1)}, bf16[4,4,2,16,1024]{4,3,2,1,0:T(8,128)(2,1)}, u32[]{:S(2)}, u32[]{:S(2)}) collective-permute-start(bf16[4,4,2,16,1024]{4,3,2,1,0:T(8,128)(2,1)S(1)} %shard_map.84), channel_id=1, source_target_pairs={{0,1},{1,0},{2,3},{3,2},{4,5},{5,4},{6,7},{7,6},{8,9},{9,8},{10,11... | collective-permute-start | bytes 3145736 | tf_op jit(solution)/shard_map/ppermute | solution.py:20
  133.0 19.4 %collective-permute-start.20 = (bf16[4,4,2,16,1024]{4,3,2,1,0:T(8,128)(2,1)S(1)}, bf16[4,4,2,16,1024]{4,3,2,1,0:T(8,128)(2,1)}, u32[]{:S(2)}, u32[]{:S(2)}) collective-permute-start(bf16[4,4,2,16,1024]{4,3,2,1,0:T(8,128)(2,1)S(1)} %shard_map.80), channel_id=1, source_target_pairs={{0,1},{1,0},{2,3},{3,2},{4,5},{5,4},{6,7},{7,6},{8,9},{9,8},{10,11... | collective-permute-start | bytes 3145736 | tf_op jit(solution)/shard_map/ppermute | solution.py:20
  155.5 18.7 %collective-permute-start.35 = (bf16[4,2,16,1024]{3,2,1,0:T(8,128)(2,1)S(1)}, bf16[4,2,16,1024]{3,2,1,0:T(8,128)(2,1)S(1)}, u32[]{:S(2)}, u32[]{:S(2)}) collective-permute-start(bf16[4,2,16,1024]{3,2,1,0:T(8,128)(2,1)S(1)} %get-tuple-element.119), channel_id=1, source_target_pairs={{0,4},{2,6},{4,0},{6,2},{1,5},{3,7},{5,1},{7,3},{8,12},{10,14},{12... | collective-permute-start | bytes 786440 | tf_op jit(solution)/shard_map/ppermute | solution.py:20
  157.3 18.3 %collective-permute-start.34 = (bf16[4,2,16,1024]{3,2,1,0:T(8,128)(2,1)S(1)}, bf16[4,2,16,1024]{3,2,1,0:T(8,128)(2,1)S(1)}, u32[]{:S(2)}, u32[]{:S(2)}) collective-permute-start(bf16[4,2,16,1024]{3,2,1,0:T(8,128)(2,1)S(1)} %get-tuple-element.120), channel_id=1, source_target_pairs={{0,2},{2,0},{4,6},{6,4},{1,3},{3,1},{5,7},{7,5},{8,10},{10,8},{12,... | collective-permute-start | bytes 786440 | tf_op jit(solution)/shard_map/ppermute | solution.py:20
  164.5 20.9 %collective-permute-start.22 = (bf16[4,2,16,1024]{3,2,1,0:T(8,128)(2,1)S(1)}, bf16[4,2,16,1024]{3,2,1,0:T(8,128)(2,1)S(1)}, u32[]{:S(2)}, u32[]{:S(2)}) collective-permute-start(bf16[4,2,16,1024]{3,2,1,0:T(8,128)(2,1)S(1)} %get-tuple-element.123), channel_id=1, source_target_pairs={{0,4},{2,6},{4,0},{6,2},{1,5},{3,7},{5,1},{7,3},{8,12},{10,14},{12... | collective-permute-start | bytes 786440 | tf_op jit(solution)/shard_map/ppermute | solution.py:20
  174.2 17.0 %collective-permute-start.10 = (bf16[4,2,16,1024]{3,2,1,0:T(8,128)(2,1)S(1)}, bf16[4,2,16,1024]{3,2,1,0:T(8,128)(2,1)S(1)}, u32[]{:S(2)}, u32[]{:S(2)}) collective-permute-start(bf16[4,2,16,1024]{3,2,1,0:T(8,128)(2,1)S(1)} %get-tuple-element.126), channel_id=1, source_target_pairs={{0,6},{2,4},{4,2},{6,0},{1,7},{3,5},{5,3},{7,1},{8,14},{10,12},{12... | collective-permute-start | bytes 786440 | tf_op jit(solution)/shard_map/ppermute | solution.py:20
  175.7 20.4 %collective-permute-start.9 = (bf16[4,2,16,1024]{3,2,1,0:T(8,128)(2,1)S(1)}, bf16[4,2,16,1024]{3,2,1,0:T(8,128)(2,1)S(1)}, u32[]{:S(2)}, u32[]{:S(2)}) collective-permute-start(bf16[4,2,16,1024]{3,2,1,0:T(8,128)(2,1)S(1)} %get-tuple-element.127), channel_id=1, source_target_pairs={{0,4},{2,6},{4,0},{6,2},{1,5},{3,7},{5,1},{7,3},{8,12},{10,14},{12... | collective-permute-start | bytes 786440 | tf_op jit(solution)/shard_map/ppermute | solution.py:20
  179.9 17.4 %collective-permute-start.8 = (bf16[4,2,16,1024]{3,2,1,0:T(8,128)(2,1)S(1)}, bf16[4,2,16,1024]{3,2,1,0:T(8,128)(2,1)S(1)}, u32[]{:S(2)}, u32[]{:S(2)}) collective-permute-start(bf16[4,2,16,1024]{3,2,1,0:T(8,128)(2,1)S(1)} %get-tuple-element.128), channel_id=1, source_target_pairs={{0,2},{2,0},{4,6},{6,4},{1,3},{3,1},{5,7},{7,5},{8,10},{10,8},{12,... | collective-permute-start | bytes 786440 | tf_op jit(solution)/shard_map/ppermute | solution.py:20
  185.6 21.4 %collective-permute-start.51 = (bf16[4,2,16,1024]{3,2,1,0:T(8,128)(2,1)S(1)}, bf16[4,2,16,1024]{3,2,1,0:T(8,128)(2,1)S(1)}, u32[]{:S(2)}, u32[]{:S(2)}) collective-permute-start(bf16[4,2,16,1024]{3,2,1,0:T(8,128)(2,1)S(1)} %get-tuple-element.102), channel_id=1, source_target_pairs={{0,16},{8,24},{16,0},{24,8},{1,17},{9,25},{17,1},{25,9},{2,18},{10... | collective-permute-start | bytes 786440 | tf_op jit(solution)/shard_map/ppermute | solution.py:20
  196.1 29.3 %collective-permute-start.37 = (bf16[4,2,16,1024]{3,2,1,0:T(8,128)(2,1)S(1)}, bf16[4,2,16,1024]{3,2,1,0:T(8,128)(2,1)S(1)}, u32[]{:S(2)}, u32[]{:S(2)}) collective-permute-start(bf16[4,2,16,1024]{3,2,1,0:T(8,128)(2,1)S(1)} %get-tuple-element.91), channel_id=1, source_target_pairs={{0,8},{8,0},{16,24},{24,16},{1,9},{9,1},{17,25},{25,17},{2,10},{10... | collective-permute-start | bytes 786440 | tf_op jit(solution)/shard_map/ppermute | solution.py:20
  197.3 43.4 %collective-permute-start.38 = (bf16[4,2,16,1024]{3,2,1,0:T(8,128)(2,1)S(1)}, bf16[4,2,16,1024]{3,2,1,0:T(8,128)(2,1)S(1)}, u32[]{:S(2)}, u32[]{:S(2)}) collective-permute-start(bf16[4,2,16,1024]{3,2,1,0:T(8,128)(2,1)S(1)} %get-tuple-element.92), channel_id=1, source_target_pairs={{0,16},{8,24},{16,0},{24,8},{1,17},{9,25},{17,1},{25,9},{2,18},{10... | collective-permute-start | bytes 786440 | tf_op jit(solution)/shard_map/ppermute | solution.py:20
  200.4 40.3 %collective-permute-start.39 = (bf16[4,2,16,1024]{3,2,1,0:T(8,128)(2,1)S(1)}, bf16[4,2,16,1024]{3,2,1,0:T(8,128)(2,1)S(1)}, u32[]{:S(2)}, u32[]{:S(2)}) collective-permute-start(bf16[4,2,16,1024]{3,2,1,0:T(8,128)(2,1)S(1)} %get-tuple-element.93), channel_id=1, source_target_pairs={{0,24},{8,16},{16,8},{24,0},{1,25},{9,17},{17,9},{25,1},{2,26},{10... | collective-permute-start | bytes 786440 | tf_op jit(solution)/shard_map/ppermute | solution.py:20
  206.9 41.0 %collective-permute-start.24 = (bf16[4,2,16,1024]{3,2,1,0:T(8,128)(2,1)S(1)}, bf16[4,2,16,1024]{3,2,1,0:T(8,128)(2,1)S(1)}, u32[]{:S(2)}, u32[]{:S(2)}) collective-permute-start(bf16[4,2,16,1024]{3,2,1,0:T(8,128)(2,1)S(1)} %get-tuple-element.81), channel_id=1, source_target_pairs={{0,8},{8,0},{16,24},{24,16},{1,9},{9,1},{17,25},{25,17},{2,10},{10... | collective-permute-start | bytes 786440 | tf_op jit(solution)/shard_map/ppermute | solution.py:20
  207.0 56.2 %collective-permute-start.25 = (bf16[4,2,16,1024]{3,2,1,0:T(8,128)(2,1)S(1)}, bf16[4,2,16,1024]{3,2,1,0:T(8,128)(2,1)S(1)}, u32[]{:S(2)}, u32[]{:S(2)}) collective-permute-start(bf16[4,2,16,1024]{3,2,1,0:T(8,128)(2,1)S(1)} %get-tuple-element.82), channel_id=1, source_target_pairs={{0,16},{8,24},{16,0},{24,8},{1,17},{9,25},{17,1},{25,9},{2,18},{10... | collective-permute-start | bytes 786440 | tf_op jit(solution)/shard_map/ppermute | solution.py:20
  225.4 37.8 %collective-permute-start.26 = (bf16[4,2,16,1024]{3,2,1,0:T(8,128)(2,1)S(1)}, bf16[4,2,16,1024]{3,2,1,0:T(8,128)(2,1)S(1)}, u32[]{:S(2)}, u32[]{:S(2)}) collective-permute-start(bf16[4,2,16,1024]{3,2,1,0:T(8,128)(2,1)S(1)} %get-tuple-element.83), channel_id=1, source_target_pairs={{0,24},{8,16},{16,8},{24,0},{1,25},{9,17},{17,9},{25,1},{2,26},{10... | collective-permute-start | bytes 786440 | tf_op jit(solution)/shard_map/ppermute | solution.py:20
  240.7 29.6 %collective-permute-start.11 = (bf16[4,2,16,1024]{3,2,1,0:T(8,128)(2,1)S(1)}, bf16[4,2,16,1024]{3,2,1,0:T(8,128)(2,1)S(1)}, u32[]{:S(2)}, u32[]{:S(2)}) collective-permute-start(bf16[4,2,16,1024]{3,2,1,0:T(8,128)(2,1)S(1)} %get-tuple-element.70), channel_id=1, source_target_pairs={{0,8},{8,0},{16,24},{24,16},{1,9},{9,1},{17,25},{25,17},{2,10},{10... | collective-permute-start | bytes 786440 | tf_op jit(solution)/shard_map/ppermute | solution.py:20
  240.7 33.7 %collective-permute-start.12 = (bf16[4,2,16,1024]{3,2,1,0:T(8,128)(2,1)S(1)}, bf16[4,2,16,1024]{3,2,1,0:T(8,128)(2,1)S(1)}, u32[]{:S(2)}, u32[]{:S(2)}) collective-permute-start(bf16[4,2,16,1024]{3,2,1,0:T(8,128)(2,1)S(1)} %get-tuple-element.71), channel_id=1, source_target_pairs={{0,16},{8,24},{16,0},{24,8},{1,17},{9,25},{17,1},{25,9},{2,18},{10... | collective-permute-start | bytes 786440 | tf_op jit(solution)/shard_map/ppermute | solution.py:20
  247.9 26.5 %collective-permute-start.13 = (bf16[4,2,16,1024]{3,2,1,0:T(8,128)(2,1)S(1)}, bf16[4,2,16,1024]{3,2,1,0:T(8,128)(2,1)S(1)}, u32[]{:S(2)}, u32[]{:S(2)}) collective-permute-start(bf16[4,2,16,1024]{3,2,1,0:T(8,128)(2,1)S(1)} %get-tuple-element.72), channel_id=1, source_target_pairs={{0,24},{8,16},{16,8},{24,0},{1,25},{9,17},{17,9},{25,1},{2,26},{10... | collective-permute-start | bytes 786440 | tf_op jit(solution)/shard_map/ppermute | solution.py:20
  (24 other events, 313.8 us)
